TPU v7x, 256 devices: a whole 4x4x8 slice. The times are simulated.
256 devices in a mesh: sector: 16 (over x, y_hi, core), term: 16 (over y_lo, z).
Axes of the slice: x: 4, y: 4 (y_hi: 2, y_lo: 2; y = y_hi * 2 + y_lo), z: 8, core: 2. Of those that a mesh axis runs over, the one named last changes fastest.
Arguments:
- x_start: float32 [16, 384, 384], P('sector', 'term'), may hold values from -6 to 6
- x_prev: float32 [16, 384, 384], P('sector', 'term'), may hold values from -6 to 6
- precond: float32 [16, 384, 384], P('sector', 'term'), may hold values from 0.5 to 6
- left_env: bfloat16 [2048, 384, 384], P(('sector', 'term')), may hold values from -0.20412415 to 1.2041241
- right_env: bfloat16 [2048, 384, 384], P(('sector', 'term')), may hold values from -0.20412415 to 1.2041241
- triples: int32 [5120, 4], P(('sector', 'term')), may hold values from 0 to 63, as said below
- trip_count: int32 [16, 16], P('sector', 'term'), may hold values from 5 to 20, as said below
- term_coef: float32 [64], replicated, may hold values from 0.25 to 1
- lanczos_beta: float32 [3], replicated, may hold values from 0.3 to 1.2
- block_owner: int32 [16], replicated, may hold values from 0 to 15, each once
Outputs:
- final_vector: float32 [16, 384, 384], P('sector', 'term')
- rayleigh: float32 [3], replicated
Inputs may be any that keep to these rules, and one draw needn't show every extreme that they name: `triples`: Columns: a left slot below 8, a wavefunction block id below 16, a right slot below 8, an operator term below 64. `trip_count`: some device has exactly 20 live triples in every draw. `block_owner`: each sector index holds exactly one block.
All inputs are finite; a program needn't handle non-finite values.
Results may differ from a plain program's by a relative error of at most 0.006.
Values may be sent and summed in bfloat16 or wider, within the bound.
A program may use at most 64 MiB of HBM per device.

v0:
```python
import functools
import math

import jax
import jax.numpy as jnp
from jax import lax
from jax.sharding import Mesh
from jax.sharding import PartitionSpec as P

APPS = 3
SECTOR = ("sector_0", "sector_1", "sector_2")
TERM = ("term_0", "term_1")
SECTOR_TERM = ("sector_0", "sector_1", "sector_2", "term_0", "term_1")


EPSILON = 1e-06


def sent_together(arrays, axis, dim, along):
    ends, at = ([], 0)
    for a in arrays[:-1]:
        at += a.shape[along]
        ends.append(at)
    both = jnp.concatenate(arrays, axis=along)
    return tuple(jnp.split(lax.all_gather(both, axis, axis=dim, tiled=True), ends, axis=along))


def in_blocks(value, dim, length):
    before, after = (value.shape[:dim], value.shape[dim + 1 :])
    return jnp.moveaxis(value.reshape(*before, length, -1, *after), dim, 0)


def summed_on_arrival(value, axis, dim):
    pieces = in_blocks(value, dim, lax.axis_size(axis))
    arrived = lax.all_to_all(pieces, axis, split_axis=0, concat_axis=0, tiled=True)
    return arrived.sum(axis=0)


def padded_to(lines, length):
    spare = -len(lines) % length
    return jnp.pad(lines, [(0, spare)] + [(0, 0)] * (lines.ndim - 1))


def joined_along(pieces, dim):
    shape = list(pieces.shape[1:])
    shape[dim] *= pieces.shape[0]
    return jnp.moveaxis(pieces, 0, dim).reshape(shape)


def copy_for_each(value, axis):
    length = lax.axis_size(axis)
    return lax.all_to_all(
        jnp.broadcast_to(value[None], (length, *value.shape)), axis, 0, 0, tiled=True
    )


def gathered_copies(value, axis, dim):
    return joined_along(copy_for_each(value, axis), dim)


def nested_sum(value, axes):
    lines = value.reshape(-1, value.shape[-1])
    own = summed_on_arrival(padded_to(lines, lax.axis_size(axes)), axes, 0)
    whole = gathered_copies(own, axes, 0)
    return whole[: len(lines)].reshape(value.shape)


def one_axis_at_a_time(value, axes):
    return functools.reduce(lax.psum, axes, value)


def local(
    x_start,
    x_prev,
    precond,
    left_env,
    right_env,
    triples,
    trip_count,
    term_coef,
    lanczos_beta,
    block_owner,
):
    sectors = lax.axis_size(SECTOR)
    term_count = lax.axis_size(TERM)
    block_size = left_env.shape[1]
    share_rows = x_start.shape[1]
    cell_count = sectors * block_size * block_size
    normaliser = 1.0 / math.sqrt(term_count * triples.shape[0])
    live_count = trip_count[0, 0]
    term_match = triples[:, 3:4] == jnp.arange(term_coef.shape[0], dtype=jnp.int32)[None, :]
    coefficient = jnp.sum(jnp.where(term_match, term_coef[None, :], 0.0), axis=1)
    owner_match = triples[:, 1:2] == jnp.arange(sectors, dtype=jnp.int32)[None, :]
    owner_rows = jnp.sum(jnp.where(owner_match, block_owner[None, :], 0), axis=1)

    def own_rows(array):
        return lax.dynamic_slice_in_dim(array, lax.axis_index(TERM) * share_rows, share_rows, 1)

    current, previous, diagonal = sent_together((x_start, x_prev, precond), TERM, 1, 0)
    quotients = []
    for position in range(APPS):
        wave_half = current.astype(jnp.bfloat16)
        gathered = lax.all_gather(wave_half, SECTOR, axis=0, tiled=True)

        def add_triple(triple, accumulated):
            left_block = lax.dynamic_index_in_dim(left_env, triples[triple, 0], 0, keepdims=False)
            wave_block = lax.dynamic_index_in_dim(gathered, owner_rows[triple], 0, keepdims=False)
            right_block = lax.dynamic_index_in_dim(right_env, triples[triple, 2], 0, keepdims=False)
            middle = jnp.dot(left_block, wave_block, preferred_element_type=jnp.float32).astype(
                jnp.bfloat16
            )
            product = jnp.dot(middle, right_block, preferred_element_type=jnp.float32)
            return accumulated + coefficient[triple] * product

        start_sum = jnp.zeros((block_size, block_size), jnp.float32)
        applied = (lax.fori_loop(0, live_count, add_triple, start_sum) * normaliser)[None]
        applied = nested_sum(applied, TERM)
        beta_now = lanczos_beta[position]
        cur_own = own_rows(current)
        app_own = own_rows(applied)
        prev_own = own_rows(previous)
        diag_own = own_rows(diagonal)
        diag_square = diag_own * diag_own
        weighted = diag_square * app_own
        weighted_cur = diag_square * cur_own
        sums_all = (
            one_axis_at_a_time(jnp.sum(cur_own * app_own), SECTOR_TERM),
            one_axis_at_a_time(jnp.sum(cur_own * cur_own), SECTOR_TERM),
            one_axis_at_a_time(jnp.sum(weighted * app_own), SECTOR_TERM),
            one_axis_at_a_time(jnp.sum(weighted * cur_own), SECTOR_TERM),
            one_axis_at_a_time(jnp.sum(weighted * prev_own), SECTOR_TERM),
            one_axis_at_a_time(jnp.sum(weighted_cur * cur_own), SECTOR_TERM),
            one_axis_at_a_time(jnp.sum(weighted_cur * prev_own), SECTOR_TERM),
            one_axis_at_a_time(jnp.sum(diag_square * prev_own * prev_own), SECTOR_TERM),
        )
        (
            cross_sum,
            self_sum,
            image_image,
            image_current,
            image_previous,
            current_current,
            current_previous,
            previous_previous,
        ) = sums_all
        quotient = cross_sum / self_sum
        square_sum = (
            image_image
            - 2.0 * quotient * image_current
            - 2.0 * beta_now * image_previous
            + quotient * quotient * current_current
            + 2.0 * quotient * beta_now * current_previous
            + beta_now * beta_now * previous_previous
        )
        residual = applied - quotient * current - beta_now * previous
        scaled = diagonal * residual
        following = scaled / jnp.sqrt(square_sum / cell_count + EPSILON)
        previous, current = (current, following)
        quotients.append(quotient)
    return (own_rows(current), jnp.stack(quotients))


def solution(mesh):
    torus = Mesh(
        mesh.devices.reshape(4, 2, 2, 2, 8),
        ("sector_0", "sector_1", "sector_2", "term_0", "term_1"),
    )
    return jax.shard_map(
        local,
        mesh=torus,
        in_specs=(
            P(SECTOR, TERM, None),
            P(SECTOR, TERM, None),
            P(SECTOR, TERM, None),
            P(SECTOR_TERM, None, None),
            P(SECTOR_TERM, None, None),
            P(SECTOR_TERM, None),
            P(SECTOR, TERM),
            P(),
            P(),
            P(),
        ),
        out_specs=(P(SECTOR, TERM, None), P()),
        check_vma=False,
    )
```

profile of v0, /device:TPU:1, one launch (start us, length us, event | category | flops | bytes accessed | tf_op | source)
XLA Modules:
  0.0 1178.0 jit_solution(13371205649114860886)
XLA Ops:
  7.2 1.4 pad_maximum_fusion
  8.7 66.4 %all-gather.5.cloned.1.call-done = f32[3,384,384]{2,1,0:T(8,128)} async-done(((f32[3,24,384]{2,1,0:T(8,128)}), f32[3,384,384]{2,1,0:T(8,128)}) %all-gather.5.cloned.1.call-update) | async-done | bytes 1769488 | tf_op jit(solution)/shard_map/all_gather | solution.py:25
  75.1 1.8 split.21
  77.7 0.8 select_reduce_fusion
  79.3 68.9 %all-gather.7.cloned.1.call-done = bf16[16,384,384]{2,1,0:T(8,128)(2,1)} async-done(((bf16[1,384,384]{2,1,0:T(8,128)(2,1)}), bf16[16,384,384]{2,1,0:T(8,128)(2,1)}) %all-gather.7.cloned.1.call-update) | async-done | bytes 4718608 | tf_op jit(solution)/shard_map/all_gather | solution.py:103
  148.3 58.2 %while.30 = (s32[]{:T(128)}, f32[384,384]{1,0:T(8,128)S(1)}, s32[]{:T(128)}, f32[20]{0:T(128)S(1)}, s32[20,4]{0,1:T(4,128)}, /*index=5*/bf16[8,384,384]{2,1,0:T(...) while((s32[]{:T(128)}, f32[384,384]{1,0:T(8,128)S(1)}, ...), condition=%wide.region_3.4_spmd, body=%wide.region_2.3_spmd.sunk | while | flops 226934800 | bytes 2065221 | solution.py:116
  148.9 1.4 constant_dynamic-slice_fusion.9
  157.3 2.4 fusion.59
  160.4 1.4 constant_dynamic-slice_fusion.9
  168.8 2.4 fusion.59
  172.0 1.4 constant_dynamic-slice_fusion.9
  180.3 2.4 fusion.59
  183.5 1.4 constant_dynamic-slice_fusion.9
  191.9 2.4 fusion.59
  195.0 1.4 constant_dynamic-slice_fusion.9
  203.4 2.4 fusion.59
  206.6 75.7 %all_to_all.30 = f32[16,24,384]{2,1,0:T(8,128)S(1)} all-to-all(f32[16,24,384]{2,1,0:T(8,128)S(1)} %bitcast.112), channel_id=1, replica_groups=mesh['sector_0'=4,'sector_1'=2,'sector_2'=2,'term_0'=2,'term_1'=8] {'ter..., dimensions={0} | all-to-all | bytes 1179648 | tf_op jit(solution)/shard_map/all_to_all | solution.py:35
  282.4 0.8 broadcast_in_dim.50
  283.2 3.6 all-to-all-start.1
  289.4 0.9 fusion.42
  290.3 7.3 all-to-all-done.1
  297.6 1.5 fusion.39
  299.1 67.6 %all-reduce.5 = (f32[]{:T(128)}, f32[]{:T(128)}, f32[]{:T(128)}, f32[]{:T(128)}, f32[]{:T(128)}, /*index=5*/f32[]{:T(128)}, f32[]{:T(128)}, f32[]{:T(128)}) all-reduce(f32[]{:T(128)} %get-tuple-element.163, f32[]{:T(128)} %get-tuple-element.166, ...), channel_id=1, replica_groups=mesh['sector_0'=4,'sector_1'=2,'sector_2'=2,'term_0'=2,'term_1'=8] {'sec..., use_global_device_ids=true, to_apply=%region_18.19 | all-reduce | flops 8 | bytes 64 | tf_op jit(solution)/shard_map/psum | solution.py:69
  366.7 26.5 %all-reduce.14 = (f32[]{:T(128)}, f32[]{:T(128)}, f32[]{:T(128)}, f32[]{:T(128)}, f32[]{:T(128)}, /*index=5*/f32[]{:T(128)}, f32[]{:T(128)}, f32[]{:T(128)}) all-reduce(f32[]{:T(128)} %get-tuple-element.261, f32[]{:T(128)} %get-tuple-element.262, ...), channel_id=1, replica_groups=mesh['sector_0'=4,'sector_1'=2,'sector_2'=2,'term_0'=2,'term_1'=8] {'sec..., use_global_device_ids=true, to_apply=%region_19.20 | all-reduce | flops 8 | bytes 64 | tf_op jit(solution)/shard_map/psum | solution.py:69
  393.2 39.6 %all-reduce.11 = (f32[]{:T(128)}, f32[]{:T(128)}, f32[]{:T(128)}, f32[]{:T(128)}, f32[]{:T(128)}, /*index=5*/f32[]{:T(128)}, f32[]{:T(128)}, f32[]{:T(128)}) all-reduce(f32[]{:T(128)} %get-tuple-element.327, f32[]{:T(128)} %get-tuple-element.328, ...), channel_id=1, replica_groups=mesh['sector_0'=4,'sector_1'=2,'sector_2'=2,'term_0'=2,'term_1'=8] {'sec..., use_global_device_ids=true, to_apply=%region_20.21 | all-reduce | flops 8 | bytes 64 | tf_op jit(solution)/shard_map/psum | solution.py:69
  432.8 4.5 all-reduce.8
  437.3 13.6 %all-reduce.2 = (f32[]{:T(128)}, f32[]{:T(128)}, f32[]{:T(128)}, f32[]{:T(128)}, f32[]{:T(128)}, /*index=5*/f32[]{:T(128)}, f32[]{:T(128)}, f32[]{:T(128)}) all-reduce(f32[]{:T(128)} %get-tuple-element.283, f32[]{:T(128)} %get-tuple-element.284, ...), channel_id=1, replica_groups=mesh['sector_0'=4,'sector_1'=2,'sector_2'=2,'term_0'=2,'term_1'=8] {'ter..., use_global_device_ids=true, to_apply=%region_22.23 | all-reduce | flops 8 | bytes 64 | tf_op jit(solution)/shard_map/psum | solution.py:69
  456.8 1.5 fusion.41
  458.2 65.9 %all-gather.9.cloned.1.call-done = bf16[16,384,384]{2,1,0:T(8,128)(2,1)} async-done(((bf16[1,384,384]{2,1,0:T(8,128)(2,1)}), bf16[16,384,384]{2,1,0:T(8,128)(2,1)}) %all-gather.9.cloned.1.call-update) | async-done | bytes 4718608 | tf_op jit(solution)/shard_map/all_gather | solution.py:103
  524.2 53.7 %while.31 = (s32[]{:T(128)}, f32[384,384]{1,0:T(8,128)S(1)}, s32[]{:T(128)}, f32[20]{0:T(128)S(1)}, s32[20,4]{0,1:T(4,128)S(1)}, /*index=5*/bf16[8,384,384]{2,1,...) while((s32[]{:T(128)}, f32[384,384]{1,0:T(8,128)S(1)}, ...), condition=%wide.region_54.55_spmd, body=%wide.region_53.54_spmd.sunk | while | flops 226934800 | bytes 2065221 | solution.py:116
  532.3 2.4 fusion.63
  543.0 2.4 fusion.63
  553.6 2.4 fusion.63
  564.2 2.4 fusion.63
  574.8 2.4 fusion.63
  578.0 71.1 %all_to_all.31 = f32[16,24,384]{2,1,0:T(8,128)S(1)} all-to-all(f32[16,24,384]{2,1,0:T(8,128)S(1)} %bitcast.113), channel_id=1, replica_groups=mesh['sector_0'=4,'sector_1'=2,'sector_2'=2,'term_0'=2,'term_1'=8] {'ter..., dimensions={0} | all-to-all | bytes 1179648 | tf_op jit(solution)/shard_map/all_to_all | solution.py:35
  649.7 1.6 broadcast_in_dim.51
  651.3 3.6 all-to-all-start.3
  657.5 8.2 all-to-all-done.3
  665.7 1.5 multiply_reduce_fusion.7
  667.2 66.4 %all-reduce.4 = (f32[]{:T(128)}, f32[]{:T(128)}, f32[]{:T(128)}, f32[]{:T(128)}, f32[]{:T(128)}, /*index=5*/f32[]{:T(128)}, f32[]{:T(128)}) all-reduce(f32[]{:T(128)} %get-tuple-element.159, f32[]{:T(128)} %get-tuple-element.160, ...), channel_id=1, replica_groups=mesh['sector_0'=4,'sector_1'=2,'sector_2'=2,'term_0'=2,'term_1'=8] {'sec..., use_global_device_ids=true, to_apply=%region_69.70 | all-reduce | flops 7 | bytes 56 | tf_op jit(solution)/shard_map/psum | solution.py:69
  733.6 21.4 %all-reduce.13 = (f32[]{:T(128)}, f32[]{:T(128)}, f32[]{:T(128)}, f32[]{:T(128)}, f32[]{:T(128)}, /*index=5*/f32[]{:T(128)}, f32[]{:T(128)}) all-reduce(f32[]{:T(128)} %get-tuple-element.254, f32[]{:T(128)} %get-tuple-element.255, ...), channel_id=1, replica_groups=mesh['sector_0'=4,'sector_1'=2,'sector_2'=2,'term_0'=2,'term_1'=8] {'sec..., use_global_device_ids=true, to_apply=%region_70.71 | all-reduce | flops 7 | bytes 56 | tf_op jit(solution)/shard_map/psum | solution.py:69
  755.1 36.9 %all-reduce.10 = (f32[]{:T(128)}, f32[]{:T(128)}, f32[]{:T(128)}, f32[]{:T(128)}, f32[]{:T(128)}, /*index=5*/f32[]{:T(128)}, f32[]{:T(128)}) all-reduce(f32[]{:T(128)} %get-tuple-element.320, f32[]{:T(128)} %get-tuple-element.321, ...), channel_id=1, replica_groups=mesh['sector_0'=4,'sector_1'=2,'sector_2'=2,'term_0'=2,'term_1'=8] {'sec..., use_global_device_ids=true, to_apply=%region_71.72 | all-reduce | flops 7 | bytes 56 | tf_op jit(solution)/shard_map/psum | solution.py:69
  792.0 4.5 all-reduce.7
  796.5 13.7 %all-reduce.1 = (f32[]{:T(128)}, f32[]{:T(128)}, f32[]{:T(128)}, f32[]{:T(128)}, f32[]{:T(128)}, /*index=5*/f32[]{:T(128)}, f32[]{:T(128)}) all-reduce(f32[]{:T(128)} %get-tuple-element.276, f32[]{:T(128)} %get-tuple-element.277, ...), channel_id=1, replica_groups=mesh['sector_0'=4,'sector_1'=2,'sector_2'=2,'term_0'=2,'term_1'=8] {'ter..., use_global_device_ids=true, to_apply=%region_73.74 | all-reduce | flops 7 | bytes 56 | tf_op jit(solution)/shard_map/psum | solution.py:69
  815.2 1.7 fusion.40
  817.0 65.9 %all-gather.11.cloned.1.call-done = bf16[16,384,384]{2,1,0:T(8,128)(2,1)} async-done(((bf16[1,384,384]{2,1,0:T(8,128)(2,1)}), bf16[16,384,384]{2,1,0:T(8,128)(2,1)}) %all-gather.11.cloned.1.call-update) | async-done | bytes 4718608 | tf_op jit(solution)/shard_map/all_gather | solution.py:103
  882.9 52.8 %while.32 = (s32[]{:T(128)}, f32[384,384]{1,0:T(8,128)S(1)}, s32[]{:T(128)}, f32[20]{0:T(128)S(1)}, s32[20,4]{0,1:T(4,128)S(1)}, /*index=5*/bf16[8,384,384]{2,1,...) while((s32[]{:T(128)}, f32[384,384]{1,0:T(8,128)S(1)}, ...), condition=%wide.region_99.100_spmd, body=%wide.region_98.99_spmd.sunk | while | flops 226934800 | bytes 2065221 | solution.py:116
  890.9 2.4 fusion.67
  901.3 2.4 fusion.67
  911.8 2.4 fusion.67
  922.2 2.4 fusion.67
  932.6 2.4 fusion.67
  935.7 70.2 %all_to_all.32 = f32[16,24,384]{2,1,0:T(8,128)S(1)} all-to-all(f32[16,24,384]{2,1,0:T(8,128)S(1)} %bitcast.114), channel_id=1, replica_groups=mesh['sector_0'=4,'sector_1'=2,'sector_2'=2,'term_0'=2,'term_1'=8] {'ter..., dimensions={0} | all-to-all | bytes 1179648 | tf_op jit(solution)/shard_map/all_to_all | solution.py:35
  1006.0 0.8 broadcast_in_dim.52
  1006.8 3.6 all-to-all-start.5
  1012.9 8.3 all-to-all-done.5
  1021.2 1.5 multiply_reduce_fusion
  1022.7 64.9 %all-reduce.3 = (f32[]{:T(128)}, f32[]{:T(128)}, f32[]{:T(128)}, f32[]{:T(128)}, f32[]{:T(128)}, /*index=5*/f32[]{:T(128)}, f32[]{:T(128)}) all-reduce(f32[]{:T(128)} %get-tuple-element.152, f32[]{:T(128)} %get-tuple-element.153, ...), channel_id=1, replica_groups=mesh['sector_0'=4,'sector_1'=2,'sector_2'=2,'term_0'=2,'term_1'=8] {'sec..., use_global_device_ids=true, to_apply=%region_114.115 | all-reduce | flops 7 | bytes 56 | tf_op jit(solution)/shard_map/psum | solution.py:69
  1087.6 21.7 %all-reduce.12 = (f32[]{:T(128)}, f32[]{:T(128)}, f32[]{:T(128)}, f32[]{:T(128)}, f32[]{:T(128)}, /*index=5*/f32[]{:T(128)}, f32[]{:T(128)}) all-reduce(f32[]{:T(128)} %get-tuple-element.247, f32[]{:T(128)} %get-tuple-element.248, ...), channel_id=1, replica_groups=mesh['sector_0'=4,'sector_1'=2,'sector_2'=2,'term_0'=2,'term_1'=8] {'sec..., use_global_device_ids=true, to_apply=%region_115.116 | all-reduce | flops 7 | bytes 56 | tf_op jit(solution)/shard_map/psum | solution.py:69
  1109.2 36.3 %all-reduce.9 = (f32[]{:T(128)}, f32[]{:T(128)}, f32[]{:T(128)}, f32[]{:T(128)}, f32[]{:T(128)}, /*index=5*/f32[]{:T(128)}, f32[]{:T(128)}) all-reduce(f32[]{:T(128)} %get-tuple-element.313, f32[]{:T(128)} %get-tuple-element.314, ...), channel_id=1, replica_groups=mesh['sector_0'=4,'sector_1'=2,'sector_2'=2,'term_0'=2,'term_1'=8] {'sec..., use_global_device_ids=true, to_apply=%region_116.117 | all-reduce | flops 7 | bytes 56 | tf_op jit(solution)/shard_map/psum | solution.py:69
  1145.6 4.5 all-reduce.6
  1150.1 13.7 %all-reduce = (f32[]{:T(128)}, f32[]{:T(128)}, f32[]{:T(128)}, f32[]{:T(128)}, f32[]{:T(128)}, /*index=5*/f32[]{:T(128)}, f32[]{:T(128)}) all-reduce(f32[]{:T(128)} %get-tuple-element.269, f32[]{:T(128)} %get-tuple-element.270, ...), channel_id=1, replica_groups=mesh['sector_0'=4,'sector_1'=2,'sector_2'=2,'term_0'=2,'term_1'=8] {'ter..., use_global_device_ids=true, to_apply=%region_118.119 | all-reduce | flops 7 | bytes 56 | tf_op jit(solution)/shard_map/psum | solution.py:69
  1168.8 2.0 multiply_divide_fusion.2
  (69 shorter events, 28.1 us)
Async XLA Ops:
  7.2 68.0 %all-gather.5.cloned.1.call-start = ((), (), s32[]{:S(2)}) async-start(), calls=%async_computation.6 | async-start | bytes 1880064 | tf_op jit(solution)/shard_map/all_gather | solution.py:25
  8.7 139.5 %all-gather.7.cloned.1.call-start = ((), (), s32[]{:S(2)}) async-start(), calls=%async_computation.7 | async-start | bytes 5013504 | tf_op jit(solution)/shard_map/all_gather | solution.py:103
  206.5 80.4 %copy-start.3 = (f32[3]{0:T(128)S(1)}, f32[3]{0:T(128)}, u32[]{:S(2)}) copy-start(f32[3]{0:T(128)} %param.24) | copy-start | bytes 40
  206.5 82.9 %copy-start = (f32[3,384,384]{2,1,0:T(8,128)S(1)}, f32[3,384,384]{2,1,0:T(8,128)}, u32[]{:S(2)}) copy-start(f32[3,384,384]{2,1,0:T(8,128)} %all-gather.5.cloned.1.call-done) | copy-start | bytes 5308420
  283.2 14.4 %all-to-all-start.1 = ((f32[16,24,384]{2,1,0:T(8,128)}), f32[16,24,384]{2,1,0:T(8,128)S(1)}, u32[]{:S(2)}, u32[]{:S(2)}) async-start(f32[16,24,384]{2,1,0:T(8,128)} %broadcast_in_dim.50), calls=%async_computation.1 | async-start | bytes 1179648 | tf_op jit(solution)/shard_map/all_to_all | solution.py:52
  286.8 237.3 %all-gather.9.cloned.1.call-start = ((), (), s32[]{:S(2)}) async-start(), calls=%async_computation.8 | async-start | bytes 5013504 | tf_op jit(solution)/shard_map/all_gather | solution.py:103
  290.3 166.4 %copy-start.1 = (f32[1,384,384]{2,1,0:T(8,128)}, f32[1,384,384]{2,1,0:T(8,128)S(1)}, u32[]{:S(2)}) copy-start(f32[1,384,384]{2,1,0:T(8,128)S(1)} %get-tuple-element.346) | copy-start | bytes 1769476
  290.3 233.9 %copy-start.2 = (s32[20,4]{0,1:T(4,128)S(1)}, s32[20,4]{0,1:T(4,128)}, u32[]{:S(2)}) copy-start(s32[20,4]{0,1:T(4,128)} %get-tuple-element.682) | copy-start | bytes 964
  651.3 14.4 %all-to-all-start.3 = ((f32[16,24,384]{2,1,0:T(8,128)}), f32[16,24,384]{2,1,0:T(8,128)S(1)}, u32[]{:S(2)}, u32[]{:S(2)}) async-start(f32[16,24,384]{2,1,0:T(8,128)} %broadcast_in_dim.51), calls=%async_computation.3 | async-start | bytes 1179648 | tf_op jit(solution)/shard_map/all_to_all | solution.py:52
  654.9 227.9 %all-gather.11.cloned.1.call-start = ((), (), s32[]{:S(2)}) async-start(), calls=%async_computation.9 | async-start | bytes 5013504 | tf_op jit(solution)/shard_map/all_gather | solution.py:103
  1006.8 14.4 %all-to-all-start.5 = ((f32[16,24,384]{2,1,0:T(8,128)}), f32[16,24,384]{2,1,0:T(8,128)S(1)}, u32[]{:S(2)}, u32[]{:S(2)}) async-start(f32[16,24,384]{2,1,0:T(8,128)} %broadcast_in_dim.52), calls=%async_computation.5 | async-start | bytes 1179648 | tf_op jit(solution)/shard_map/all_to_all | solution.py:52
Sparse Core Ops, SparseCore 0:
  9.8 65.2 all-gather.4
  77.8 70.3 all-gather.6
  458.4 65.7 all-gather.8
  817.1 65.7 all-gather.10
where the time goes:
time: 1190 us; the launch traced here: 1180 us
  blocking collectives  653 us (55%)
  waiting for transfers between devices  291 us (24%)
  loops' own time  97.1 us (8%)
  local copies, waits for them, and re-layouts  38.8 us (3%)
  between operations  36.8 us (3%)
  matrix products  36.4 us (3%)
  other arithmetic  14.2 us (1%)
    psum x15, blocking collectives, one_axis_at_a_time(): return functools.reduce(lax.psum, axes, value)  436 us
    all_to_all x3, blocking collectives, summed_on_arrival(): lax.all_to_all(pieces, axis, split_axis=0, concat_axis=0, tiled=True)  217 us
    all_gather x3, waiting for transfers between devices, local(): gathered = lax.all_gather(wave_half, SECTOR, axis=0, tiled=True)  201 us
    another operation x3, loops' own time, local(): lax.fori_loop(0, live_count, add_triple, start_sum) * normaliser  97.1 us
    all_gather x1, waiting for transfers between devices, sent_together(): lax.all_gather(both, axis, axis=dim, tiled=True)  66.4 us
    dot_general x15, matrix products, add_triple(): product = jnp.dot(middle, right_block, preferred_element_type=jnp.float32)  36.4 us
  transfers between devices with their start and end apart: 7, of which 7 were waited for; matrix products, arithmetic and copies ran while one was open for 0% of the time, Pallas kernels for 0%

commit v1 on v0

v1 whole, which is shorter than its diff:
```python
import functools
import math

import jax
import jax.numpy as jnp
from jax import lax
from jax.experimental import pallas as pl
from jax.experimental.pallas import tpu as pltpu
from jax.sharding import Mesh
from jax.sharding import PartitionSpec as P

APPS = 3
B = 384
TRIP = 20
SHARE = 24
PIECE = 192
HALF = 96
GROUP = 4
SECTOR = ("x", "yh", "c")
TERM = ("yl", "z")
ALL = ("x", "yh", "c", "yl", "z")
EPSILON = 1e-06
MESH = pl.DeviceIdType.MESH
OFFSETS = (0, -1, 1, 2)


def kernel(
    x_ref,
    xp_ref,
    d_ref,
    left_hbm,
    right_hbm,
    triples,
    count,
    coef,
    beta,
    owner,
    out_ref,
    ray_ref,
    left,
    right,
    wave,
    mid,
    img,
    pimg,
    rsbuf,
    zimg,
    zcur,
    zprev,
    zdiag,
    cur,
    prev,
    sabuf,
    sbbuf,
    env_sem,
    g_send,
    g_recv,
    b_send,
    b_recv,
    r_send,
    r_recv,
    sa_send,
    sa_recv,
    sb_send,
    sb_recv,
    z_send,
    z_recv,
    i_send,
    i_recv,
):
    x = lax.axis_index("x")
    yh = lax.axis_index("yh")
    c = lax.axis_index("c")
    yl = lax.axis_index("yl")
    z = lax.axis_index("z")
    y = yh * 2 + yl
    sector = (x * 2 + yh) * 2 + c
    term = yl * 8 + z
    p = (1 - c) * y + c * x
    q = (1 - c) * x + c * y

    def device(nx, ny, nc, nz):
        return {"x": nx, "yh": ny // 2, "c": nc, "yl": ny % 2, "z": nz}

    def along_p(d):
        return device((x + c * d + 4) % 4, (y + (1 - c) * d + 4) % 4, c, z)

    def along_q(d):
        return device((x + (1 - c) * d + 4) % 4, (y + c * d + 4) % 4, c, z)

    def term_peer(dyl, dz):
        return {"x": x, "yh": yh, "c": c, "yl": (yl + dyl) % 2, "z": (z + dz) % 8}

    def sector_peer(dx, dyh, dc):
        return {"x": (x + dx) % 4, "yh": (yh + dyh) % 2, "c": (c + dc) % 2, "yl": yl, "z": z}

    term_offsets = [(o // 8, o % 8) for o in range(1, 16)]
    sector_offsets = [(o // 4, (o // 2) % 2, o % 2) for o in range(1, 16)]
    sibling = sector_peer(0, 0, 1)

    def remote(src, dst, send, recv, dev):
        return pltpu.make_async_remote_copy(
            src_ref=src, dst_ref=dst, send_sem=send, recv_sem=recv, device_id=dev, device_id_type=MESH
        )

    env = [
        pltpu.make_async_copy(left_hbm, left, env_sem.at[0]),
        pltpu.make_async_copy(right_hbm, right, env_sem.at[1]),
    ]
    for e in env:
        e.start()

    barrier = pltpu.get_barrier_semaphore()
    peers = [term_peer(*o) for o in term_offsets] + [sector_peer(*o) for o in sector_offsets]
    peers.append({"x": x, "yh": 1 - yh, "c": c, "yl": 1 - yl, "z": z})
    for dev in peers:
        pl.semaphore_signal(barrier, inc=1, device_id=dev, device_id_type=MESH)
    my_rows = pl.ds(pl.multiple_of(SHARE * term, 8), SHARE)
    cur[...] = x_ref[0]
    prev[...] = xp_ref[0]
    zcur[z] = x_ref[0]
    zprev[z] = xp_ref[0]
    zdiag[z] = d_ref[0]
    zimg[z] = x_ref[0].astype(jnp.bfloat16)
    pl.semaphore_wait(barrier, len(peers))

    def z_copy(dz):
        mine = zimg.at[z]
        return remote(mine, mine, z_send.at[dz], z_recv.at[dz], term_peer(0, dz))

    def z_arrival(dz):
        theirs = zimg.at[(z - dz + 8) % 8]
        return remote(theirs, theirs, z_send.at[dz], z_recv.at[dz], term_peer(0, dz))

    def state_copy(n, ref, dz):
        mine = ref.at[z]
        return remote(mine, mine, i_send.at[n, dz], i_recv.at[n, dz], term_peer(0, dz))

    def state_arrival(n, ref, dz):
        theirs = ref.at[(z - dz + 8) % 8]
        return remote(theirs, theirs, i_send.at[n, dz], i_recv.at[n, dz], term_peer(0, dz))

    states = ((0, zcur), (1, zprev), (2, zdiag))
    for dz in range(1, 8):
        z_copy(dz).start()
    for n, ref in states:
        for dz in range(1, 8):
            state_copy(n, ref, dz).start()
    for dz in range(1, 8):
        z_copy(dz).wait_send()
        z_arrival(dz).wait_recv()

    def set_wave(value):
        rows = pl.ds(pl.multiple_of(PIECE * yl, 64), PIECE)
        wave[sector, rows, :] = value.reshape(PIECE, B).astype(jnp.bfloat16)

    set_wave(zimg[...].astype(jnp.float32))

    def piece_at(px, py, core, start, length):
        block = (px * 2 + py // 2) * 2 + core
        rows = pl.multiple_of((py % 2) * PIECE + start, 32)
        return wave.at[block, pl.ds(rows, length)]

    def piece(a, b, start=0, length=PIECE):
        a, b = (a + 4) % 4, (b + 4) % 4
        return piece_at((1 - c) * b + c * a, (1 - c) * a + c * b, c, start, length)

    def p_copy(k):
        where = (piece(p, q), piece(p, q), piece(p - 1, q, 0, HALF), piece(p + 1, q, HALF, HALF))[k]
        dev = along_p(1 if k % 2 == 0 else -1)
        return remote(where, where, g_send.at[k], g_recv.at[k], dev)

    def p_arrival(k):
        where = (piece(p - 1, q), piece(p + 1, q), piece(p - 2, q, 0, HALF), piece(p + 2, q, HALF, HALF))[k]
        dev = along_p(1 if k % 2 == 0 else -1)
        return remote(where, where, g_send.at[k], g_recv.at[k], dev)

    def q_copy(j, k):
        a = p + OFFSETS[j]
        where = (piece(a, q), piece(a, q), piece(a, q - 1, 0, HALF), piece(a, q + 1, HALF, HALF))[k]
        dev = along_q(1 if k % 2 == 0 else -1)
        n = 4 + 4 * j + k
        return remote(where, where, g_send.at[n], g_recv.at[n], dev)

    def q_arrival(j, k):
        a = p + OFFSETS[j]
        where = (piece(a, q - 1), piece(a, q + 1), piece(a, q - 2, 0, HALF), piece(a, q + 2, HALF, HALF))[k]
        dev = along_q(1 if k % 2 == 0 else -1)
        n = 4 + 4 * j + k
        return remote(where, where, g_send.at[n], g_recv.at[n], dev)

    def to_sibling(a, b):
        a, b = (a + 4) % 4, (b + 4) % 4
        px, py = (1 - c) * b + c * a, (1 - c) * a + c * b
        where = piece_at(px, py, c, 0, PIECE)
        n = px * 4 + py
        return remote(where, where, b_send.at[n], b_recv.at[n], sibling)

    def from_sibling(n):
        where = piece_at(n // 4, n % 4, 1 - c, 0, PIECE)
        return remote(where, where, b_send.at[n], b_recv.at[n], sibling)

    def sent_to_sibling(n):
        where = piece_at(n // 4, n % 4, c, 0, PIECE)
        return remote(where, where, b_send.at[n], b_recv.at[n], sibling)

    def gather():
        p_copy(0).start()
        p_copy(1).start()
        q_copy(0, 0).start()
        q_copy(0, 1).start()
        to_sibling(p, q).start()
        for k in (0, 1):
            p_arrival(k).wait_recv()
            p_copy(2 + k).start()
        for j in (1, 2):
            q_copy(j, 0).start()
            q_copy(j, 1).start()
            to_sibling(p + OFFSETS[j], q).start()

        def neighbours(j):
            for k in (0, 1):
                q_arrival(j, k).wait_recv()
                q_copy(j, 2 + k).start()
            to_sibling(p + OFFSETS[j], q - 1).start()
            to_sibling(p + OFFSETS[j], q + 1).start()

        neighbours(0)
        p_arrival(2).wait_recv()
        p_arrival(3).wait_recv()
        q_copy(3, 0).start()
        q_copy(3, 1).start()
        to_sibling(p + 2, q).start()

        def opposite(j):
            q_arrival(j, 2).wait_recv()
            q_arrival(j, 3).wait_recv()
            to_sibling(p + OFFSETS[j], q + 2).start()

        neighbours(1)
        neighbours(2)
        opposite(0)
        neighbours(3)
        opposite(1)
        opposite(2)
        opposite(3)
        for k in range(4):
            p_copy(k).wait_send()
        for j in range(4):
            for k in range(4):
                q_copy(j, k).wait_send()
        for n in range(16):
            from_sibling(n).wait_recv()
        for n in range(16):
            sent_to_sibling(n).wait_send()

    live = count[0, 0]
    normaliser = 1.0 / math.sqrt(16 * TRIP)

    def compute():
        img[...] = jnp.zeros_like(img)

        def step(g, carry):
            for j in range(GROUP):
                k = g * GROUP + j
                weight = jnp.where(k < live, coef[triples[k, 3]] * normaliser, 0.0)
                m = jnp.dot(
                    left[triples[k, 0]], wave[owner[triples[k, 1]]], preferred_element_type=jnp.float32
                )
                mid[:, j * B : (j + 1) * B] = (m * weight).astype(jnp.bfloat16)
            rights = jnp.concatenate([right[triples[g * GROUP + j, 2]] for j in range(GROUP)], axis=0)
            img[...] += jnp.dot(mid[...], rights, preferred_element_type=jnp.float32)
            return carry

        lax.fori_loop(0, TRIP // GROUP, step, 0)
        pimg[...] = img[...].reshape(16, SHARE, B).astype(jnp.bfloat16)

    def index_of(dyl, dz):
        return dyl * 8 + dz

    def rs_copy(dyl, dz):
        to = ((yl + dyl) % 2) * 8 + (z + dz) % 8
        o = index_of(dyl, dz)
        return remote(pimg.at[to], rsbuf.at[term], r_send.at[o], r_recv.at[o], term_peer(dyl, dz))

    def rs_arrival(dyl, dz):
        sender = ((yl + dyl) % 2) * 8 + (z - dz + 8) % 8
        o = index_of(dyl, dz)
        return remote(rsbuf.at[sender], rsbuf.at[sender], r_send.at[o], r_recv.at[o], term_peer(dyl, dz))

    def sa_copy(dyl, dz):
        o = index_of(dyl, dz)
        mine = sabuf.at[term]
        return remote(mine, mine, sa_send.at[o], sa_recv.at[o], term_peer(dyl, dz))

    def sa_arrival(dyl, dz):
        o = index_of(dyl, dz)
        theirs = sabuf.at[((yl + dyl) % 2) * 8 + (z - dz + 8) % 8]
        return remote(theirs, theirs, sa_send.at[o], sa_recv.at[o], term_peer(dyl, dz))

    def sb_copy(dx, dyh, dc):
        o = dx * 4 + dyh * 2 + dc
        mine = sbbuf.at[sector]
        return remote(mine, mine, sb_send.at[o], sb_recv.at[o], sector_peer(dx, dyh, dc))

    def sb_arrival(dx, dyh, dc):
        o = dx * 4 + dyh * 2 + dc
        theirs = sbbuf.at[(((x - dx + 4) % 4) * 2 + (yh + dyh) % 2) * 2 + (c + dc) % 2]
        return remote(theirs, theirs, sb_send.at[o], sb_recv.at[o], sector_peer(dx, dyh, dc))

    for e in env:
        e.wait()

    def application(i, carry):
        gather()
        compute()
        for o in term_offsets:
            rs_copy(*o).start()
        rsbuf[term] = jnp.zeros((SHARE, B), jnp.bfloat16)
        for o in term_offsets:
            rs_arrival(*o).wait_recv()
        for o in term_offsets:
            rs_copy(*o).wait_send()
        image = img[my_rows, :]
        for t in range(16):
            image = image + rsbuf[t].astype(jnp.float32)
        now = cur[...]
        before = prev[...]
        square = d_ref[0] * d_ref[0]
        weighted = square * image
        weighted_now = square * now
        products = (
            now * image,
            now * now,
            weighted * image,
            weighted * now,
            weighted * before,
            weighted_now * now,
            weighted_now * before,
            square * before * before,
        )

        def lanes(value):
            rows = jnp.sum(value, axis=0, keepdims=True)
            return rows[:, :128] + rows[:, 128:256] + rows[:, 256:]

        sabuf[term] = jnp.concatenate([lanes(v) for v in products], axis=0)
        for o in term_offsets:
            sa_copy(*o).start()

        @pl.when(i < APPS - 1)
        def _():
            zimg[z] = image.astype(jnp.bfloat16)
            for dz in range(1, 8):
                z_copy(dz).start()

        for o in term_offsets:
            sa_arrival(*o).wait_recv()
        sbbuf[sector] = jnp.sum(sabuf[...], axis=0)
        for o in sector_offsets:
            sb_copy(*o).start()
        for o in sector_offsets:
            sb_arrival(*o).wait_recv()
        for o in term_offsets:
            sa_copy(*o).wait_send()
        for o in sector_offsets:
            sb_copy(*o).wait_send()
        totals = jnp.sum(jnp.sum(sbbuf[...], axis=0), axis=1, keepdims=True)
        cross, self_, ii, ic, ip, cc, cp, pp = [totals[j : j + 1] for j in range(8)]
        beta_now = beta[i]
        quotient = cross / self_
        squares = (
            ii
            - 2.0 * quotient * ic
            - 2.0 * beta_now * ip
            + quotient * quotient * cc
            + 2.0 * quotient * beta_now * cp
            + beta_now * beta_now * pp
        )
        inverse = 1.0 / jnp.sqrt(squares / (16 * B * B) + EPSILON)
        ray_ref[i] = jnp.sum(quotient)

        @pl.when(i < APPS - 1)
        def _():
            @pl.when(i == 0)
            def _():
                for n, ref in states:
                    for dz in range(1, 8):
                        state_arrival(n, ref, dz).wait_recv()
                        state_copy(n, ref, dz).wait_send()

            for dz in range(1, 8):
                z_arrival(dz).wait_recv()
                z_copy(dz).wait_send()
            znow = zcur[...]
            znext = zdiag[...] * (zimg[...].astype(jnp.float32) - quotient * znow - beta_now * zprev[...]) * inverse
            zprev[...] = znow
            zcur[...] = znext
            set_wave(znext)

        following = d_ref[0] * (image - quotient * now - beta_now * before) * inverse
        prev[...] = now
        cur[...] = following
        return carry

    lax.fori_loop(0, APPS, application, 0)
    out_ref[0] = cur[...]


def local(x_start, x_prev, precond, left_env, right_env, triples, trip_count, term_coef, lanczos_beta, block_owner):
    vmem = pl.BlockSpec(memory_space=pltpu.VMEM)
    smem = pl.BlockSpec(memory_space=pltpu.SMEM)
    hbm = pl.BlockSpec(memory_space=pl.ANY)
    dma = pltpu.SemaphoreType.DMA
    f32, bf16 = jnp.float32, jnp.bfloat16
    return pl.pallas_call(
        kernel,
        out_shape=(jax.ShapeDtypeStruct((1, SHARE, B), f32), jax.ShapeDtypeStruct((APPS,), f32)),
        in_specs=[vmem, vmem, vmem, hbm, hbm, smem, smem, smem, smem, smem],
        out_specs=(vmem, smem),
        scratch_shapes=[
            pltpu.VMEM((8, B, B), bf16),
            pltpu.VMEM((8, B, B), bf16),
            pltpu.VMEM((16, B, B), bf16),
            pltpu.VMEM((B, GROUP * B), bf16),
            pltpu.VMEM((B, B), f32),
            pltpu.VMEM((16, SHARE, B), bf16),
            pltpu.VMEM((16, SHARE, B), bf16),
            pltpu.VMEM((8, SHARE, B), bf16),
            pltpu.VMEM((8, SHARE, B), f32),
            pltpu.VMEM((8, SHARE, B), f32),
            pltpu.VMEM((8, SHARE, B), f32),
            pltpu.VMEM((SHARE, B), f32),
            pltpu.VMEM((SHARE, B), f32),
            pltpu.VMEM((16, 8, 128), f32),
            pltpu.VMEM((16, 8, 128), f32),
            dma((2,)),
            dma((20,)),
            dma((20,)),
            dma((16,)),
            dma((16,)),
            dma((16,)),
            dma((16,)),
            dma((16,)),
            dma((16,)),
            dma((16,)),
            dma((16,)),
            dma((8,)),
            dma((8,)),
            dma((3, 8)),
            dma((3, 8)),
        ],
        compiler_params=pltpu.CompilerParams(
            collective_id=0, has_side_effects=True, vmem_limit_bytes=48 * 2**20
        ),
        name="window",
    )(x_start, x_prev, precond, left_env, right_env, triples, trip_count, term_coef, lanczos_beta, block_owner)


def solution(mesh):
    torus = Mesh(mesh.devices.reshape(4, 2, 2, 2, 8), ALL)
    return jax.shard_map(
        local,
        mesh=torus,
        in_specs=(
            P(SECTOR, TERM, None),
            P(SECTOR, TERM, None),
            P(SECTOR, TERM, None),
            P(ALL, None, None),
            P(ALL, None, None),
            P(ALL, None),
            P(SECTOR, TERM),
            P(),
            P(),
            P(),
        ),
        out_specs=(P(SECTOR, TERM, None), P()),
        check_vma=False,
    )
```

time: 1190 us -> 181 us (0.15); the launches traced: 1180 us -> 181 us
  blocking collectives: 653 us -> 0 us
  waiting for transfers between devices: 291 us -> 0 us
  Pallas kernels: 0 us -> 170 us
  loops' own time: 97.1 us -> 0 us
  matrix products: 36.4 us -> 0 us
  between operations: 36.8 us -> 1.29 us
  local copies, waits for them, and re-layouts: 38.8 us -> 9.5 us
  other arithmetic: 14.2 us -> 0 us
    psum x15 -> x0, blocking collectives: 436 us -> none  [one_axis_at_a_time(): return functools.reduce(lax.psum, axes, value)]
    all_gather x4 -> x0, waiting for transfers between devices: 267 us -> none  [the longest x3 201 us: local(): gathered = lax.all_gather(wave_half, SECTOR, axis=0, tiled=True)]
    all_to_all x3 -> x0, blocking collectives: 217 us -> none  [summed_on_arrival(): lax.all_to_all(pieces, axis, split_axis=0, concat_axis=0, tiled=True)]
    pallas_call x0 -> x1, Pallas kernels: none -> 170 us  [local(): pl.pallas_call(kernel, out_shape=(jax.ShapeDtypeStruct((1, SHARE, B), f32...]
    another operation x3 -> x0, loops' own time: 97.1 us -> none  [local(): lax.fori_loop(0, live_count, add_triple, start_sum) * normaliser]
    dot_general x15 -> x0, matrix products: 36.4 us -> none  [add_triple(): product = jnp.dot(middle, right_block, preferred_element_type=jnp.float32)]
    dynamic_slice x45 -> x0, local copies, waits for them, and re-layouts: 31.2 us -> none  [the longest x15 13.2 us: add_triple(): triples[triple, 0]]
    all_to_all x3 -> x0, waiting for transfers between devices: 23.8 us -> none  [copy_for_each(): lax.all_to_all(jnp.broadcast_to(value[None], (length, *value.shape)), axi...]
  transfers between devices with their start and end apart: 7 -> 0, of which waited for: 7 -> 0; matrix products, arithmetic and copies ran while one was open for 0% -> 0% of each run, Pallas kernels for 0% -> 0%
where the time goes in v1:
time: 181 us
  Pallas kernels  170 us (94%)
  local copies, waits for them, and re-layouts  9.5 us (5%)
    pallas_call x1, Pallas kernels, local(): pl.pallas_call(kernel, out_shape=(jax.ShapeDtypeStruct((1, SHARE, B), f32...  170 us
    unnamed x19, local copies, waits for them, and re-layouts  9.5 us

profile of v1, /device:TPU:1, one launch (start us, length us, event | category | flops | bytes accessed | tf_op | source)
XLA Modules:
  0.0 181.0 jit_solution(17838221663220794468)
XLA Ops:
  1.3 0.8 copy.12.triples
  2.0 0.0 copy-start
  2.1 1.7 copy-done
  3.7 0.0 copy-start.1
  3.7 1.7 copy-done.1
  5.4 0.0 copy-start.2
  5.4 0.8 copy-done.2
  6.1 0.0 copy-start.3
  6.2 0.8 copy-done.3
  6.9 0.0 copy-start.4
  6.9 0.8 copy-done.4
  7.7 0.0 copy-start.5
  7.7 0.7 copy-done.5
  8.3 0.0 copy-start.6
  8.3 0.7 copy-done.6
  9.0 0.0 copy-start.7
  9.0 0.7 copy-done.7
  9.7 170.2 %window.1 = (f32[1,24,384]{2,1,0:T(8,128)S(1)}, f32[3]{0:T(128)S(1)}) custom-call(f32[1,24,384]{2,1,0:T(8,128)S(1)} %copy-done.2, f32[1,24,384]{2,1,0:T(8,128)S(1)} %copy-done.3, f32[1,24,384]{2,1,0:T(8,128)S(1)} %copy-done.4, bf16[8,384,384]{2,1,0:T(8,128)(2,1)S(1)} %copy-done, bf16[8,384,384]{2,1,0:T(8,128)(2,1)S(1)} %copy-done.1, ...), custom_call_target="tpu_custom_call" | custom-call | tf_op jit(solution)/shard_map/window/pallas_call | solution.py:416
  179.9 0.6 copy.16
  180.5 0.5 copy.17
Async XLA Ops:
  2.0 1.7 copy-start
  3.7 1.7 copy-start.1
  5.4 0.8 copy-start.2
  6.1 0.8 copy-start.3
  6.9 0.8 copy-start.4
  7.7 0.7 copy-start.5
  8.3 0.7 copy-start.6
  9.0 0.7 copy-start.7

commit v2 on v1

v2 whole, which is shorter than its diff:
```python
import functools
import math

import jax
import jax.numpy as jnp
from jax import lax
from jax.experimental import pallas as pl
from jax.experimental.pallas import tpu as pltpu
from jax.sharding import Mesh
from jax.sharding import PartitionSpec as P

APPS = 3
B = 384
TRIP = 20
SHARE = 24
PIECE = 192
HALF = 96
GROUP = 4
SECTOR = ("x", "yh", "c")
TERM = ("yl", "z")
ALL = ("x", "yh", "c", "yl", "z")
EPSILON = 1e-06
MESH = pl.DeviceIdType.MESH
OFFSETS = (0, -1, 1, 2)


def kernel(
    x_hbm,
    xp_hbm,
    d_hbm,
    left_hbm,
    right_hbm,
    triples_hbm,
    count_hbm,
    coef_hbm,
    beta_hbm,
    owner_hbm,
    out_ref,
    ray_ref,
    left,
    right,
    wave,
    mid,
    img,
    pimg,
    rsbuf,
    zimg,
    cur,
    prev,
    diag,
    qabuf,
    qbbuf,
    nabuf,
    nbbuf,
    triples,
    count,
    coef,
    beta,
    owner,
    in_sem,
    g_send,
    g_recv,
    b_send,
    b_recv,
    r_send,
    r_recv,
    z_send,
    z_recv,
    s_send,
    s_recv,
):
    x = lax.axis_index("x")
    yh = lax.axis_index("yh")
    c = lax.axis_index("c")
    yl = lax.axis_index("yl")
    z = lax.axis_index("z")
    y = yh * 2 + yl
    sector = (x * 2 + yh) * 2 + c
    term = yl * 8 + z
    p = (1 - c) * y + c * x
    q = (1 - c) * x + c * y

    def device(nx, ny, nc, nz):
        return {"x": nx, "yh": ny // 2, "c": nc, "yl": ny % 2, "z": nz}

    def along_p(d):
        return device((x + c * d + 4) % 4, (y + (1 - c) * d + 4) % 4, c, z)

    def along_q(d):
        return device((x + (1 - c) * d + 4) % 4, (y + c * d + 4) % 4, c, z)

    def term_peer(dyl, dz):
        return {"x": x, "yh": yh, "c": c, "yl": (yl + dyl) % 2, "z": (z + dz) % 8}

    def sector_peer(dx, dyh, dc):
        return {"x": (x + dx) % 4, "yh": (yh + dyh) % 2, "c": (c + dc) % 2, "yl": yl, "z": z}

    term_offsets = [(o // 8, o % 8) for o in range(1, 16)]
    sector_offsets = [(o // 4, (o // 2) % 2, o % 2) for o in range(1, 16)]
    sibling = sector_peer(0, 0, 1)

    def remote(src, dst, send, recv, dev):
        return pltpu.make_async_remote_copy(
            src_ref=src, dst_ref=dst, send_sem=send, recv_sem=recv, device_id=dev, device_id_type=MESH
        )

    moves = [
        pltpu.make_async_copy(src, dst, in_sem.at[n])
        for n, (src, dst) in enumerate(
            (
                (x_hbm.at[0], cur),
                (xp_hbm.at[0], prev),
                (d_hbm.at[0], diag),
                (triples_hbm, triples),
                (count_hbm, count),
                (coef_hbm, coef),
                (beta_hbm, beta),
                (owner_hbm, owner),
                (left_hbm, left),
                (right_hbm, right),
            )
        )
    ]
    for move in moves:
        move.start()

    barrier = pltpu.get_barrier_semaphore()
    peers = [term_peer(*o) for o in term_offsets] + [sector_peer(*o) for o in sector_offsets]
    peers.append({"x": x, "yh": 1 - yh, "c": c, "yl": 1 - yl, "z": z})
    for dev in peers:
        pl.semaphore_signal(barrier, inc=1, device_id=dev, device_id_type=MESH)
    my_rows = pl.ds(pl.multiple_of(SHARE * term, 8), SHARE)
    moves[0].wait()
    zimg[z] = cur[...].astype(jnp.bfloat16)
    pl.semaphore_wait(barrier, len(peers))

    def z_copy(dz):
        mine = zimg.at[z]
        return remote(mine, mine, z_send.at[dz], z_recv.at[dz], term_peer(0, dz))

    def z_arrival(dz):
        theirs = zimg.at[(z - dz + 8) % 8]
        return remote(theirs, theirs, z_send.at[dz], z_recv.at[dz], term_peer(0, dz))

    def z_start():
        for dz in range(1, 8):
            z_copy(dz).start()

    def set_wave(value):
        rows = pl.ds(pl.multiple_of(PIECE * yl, 64), PIECE)
        wave[sector, rows, :] = value.reshape(PIECE, B).astype(jnp.bfloat16)

    def piece_at(px, py, core, start, length):
        block = (px * 2 + py // 2) * 2 + core
        rows = pl.multiple_of((py % 2) * PIECE + start, 32)
        return wave.at[block, pl.ds(rows, length)]

    def piece(a, b, start=0, length=PIECE):
        a, b = (a + 4) % 4, (b + 4) % 4
        return piece_at((1 - c) * b + c * a, (1 - c) * a + c * b, c, start, length)

    def p_copy(k):
        where = (piece(p, q), piece(p, q), piece(p - 1, q, 0, HALF), piece(p + 1, q, HALF, HALF))[k]
        dev = along_p(1 if k % 2 == 0 else -1)
        return remote(where, where, g_send.at[k], g_recv.at[k], dev)

    def p_arrival(k):
        where = (piece(p - 1, q), piece(p + 1, q), piece(p - 2, q, 0, HALF), piece(p + 2, q, HALF, HALF))[k]
        dev = along_p(1 if k % 2 == 0 else -1)
        return remote(where, where, g_send.at[k], g_recv.at[k], dev)

    def q_copy(j, k):
        a = p + OFFSETS[j]
        where = (piece(a, q), piece(a, q), piece(a, q - 1, 0, HALF), piece(a, q + 1, HALF, HALF))[k]
        dev = along_q(1 if k % 2 == 0 else -1)
        n = 4 + 4 * j + k
        return remote(where, where, g_send.at[n], g_recv.at[n], dev)

    def q_arrival(j, k):
        a = p + OFFSETS[j]
        where = (piece(a, q - 1), piece(a, q + 1), piece(a, q - 2, 0, HALF), piece(a, q + 2, HALF, HALF))[k]
        dev = along_q(1 if k % 2 == 0 else -1)
        n = 4 + 4 * j + k
        return remote(where, where, g_send.at[n], g_recv.at[n], dev)

    def to_sibling(a, b):
        a, b = (a + 4) % 4, (b + 4) % 4
        px, py = (1 - c) * b + c * a, (1 - c) * a + c * b
        where = piece_at(px, py, c, 0, PIECE)
        n = px * 4 + py
        return remote(where, where, b_send.at[n], b_recv.at[n], sibling)

    def from_sibling(n):
        where = piece_at(n // 4, n % 4, 1 - c, 0, PIECE)
        return remote(where, where, b_send.at[n], b_recv.at[n], sibling)

    def sent_to_sibling(n):
        where = piece_at(n // 4, n % 4, c, 0, PIECE)
        return remote(where, where, b_send.at[n], b_recv.at[n], sibling)

    def gather(beside):
        p_copy(0).start()
        p_copy(1).start()
        q_copy(0, 0).start()
        q_copy(0, 1).start()
        to_sibling(p, q).start()
        for k in (0, 1):
            p_arrival(k).wait_recv()
            p_copy(2 + k).start()
        for j in (1, 2):
            q_copy(j, 0).start()
            q_copy(j, 1).start()
            to_sibling(p + OFFSETS[j], q).start()

        def neighbours(j):
            for k in (0, 1):
                q_arrival(j, k).wait_recv()
                q_copy(j, 2 + k).start()
            to_sibling(p + OFFSETS[j], q - 1).start()
            to_sibling(p + OFFSETS[j], q + 1).start()

        neighbours(0)
        p_arrival(2).wait_recv()
        p_arrival(3).wait_recv()
        q_copy(3, 0).start()
        q_copy(3, 1).start()
        to_sibling(p + 2, q).start()

        def opposite(j):
            q_arrival(j, 2).wait_recv()
            q_arrival(j, 3).wait_recv()
            to_sibling(p + OFFSETS[j], q + 2).start()

        neighbours(1)
        neighbours(2)
        beside()
        opposite(0)
        neighbours(3)
        opposite(1)
        opposite(2)
        opposite(3)
        for k in range(4):
            p_copy(k).wait_send()
        for j in range(4):
            for k in range(4):
                q_copy(j, k).wait_send()
        for n in range(16):
            from_sibling(n).wait_recv()
        for n in range(16):
            sent_to_sibling(n).wait_send()

    normaliser = 1.0 / math.sqrt(16 * TRIP)

    def compute():
        live = count[0]
        img[...] = jnp.zeros_like(img)

        def step(g, carry):
            for j in range(GROUP):
                k = g * GROUP + j
                weight = jnp.where(k < live, coef[triples[3, k]] * normaliser, 0.0)
                m = jnp.dot(
                    left[triples[0, k]], wave[owner[triples[1, k]]], preferred_element_type=jnp.float32
                )
                mid[:, j * B : (j + 1) * B] = (m * weight).astype(jnp.bfloat16)
            rights = jnp.concatenate([right[triples[2, g * GROUP + j]] for j in range(GROUP)], axis=0)
            img[...] += jnp.dot(mid[...], rights, preferred_element_type=jnp.float32)
            return carry

        lax.fori_loop(0, TRIP // GROUP, step, 0)

    def rs_copy(dyl, dz):
        to = ((yl + dyl) % 2) * 8 + (z + dz) % 8
        o = dyl * 8 + dz
        return remote(pimg.at[to], rsbuf.at[term], r_send.at[o], r_recv.at[o], term_peer(dyl, dz))

    def rs_arrival(dyl, dz):
        sender = ((yl + dyl) % 2) * 8 + (z - dz + 8) % 8
        o = dyl * 8 + dz
        return remote(rsbuf.at[sender], rsbuf.at[sender], r_send.at[o], r_recv.at[o], term_peer(dyl, dz))

    def spread(value):
        rows = jnp.sum(value.reshape(-1, 8, B), axis=0)
        return rows[:, :128] + rows[:, 128:256] + rows[:, 256:]

    def first_hop(buf, n, dyl, dz, arrival):
        o = dyl * 8 + dz
        slot = ((yl + dyl) % 2) * 8 + (z - dz + 8) % 8 if arrival else term
        ref = buf.at[slot]
        return remote(ref, ref, s_send.at[n, o], s_recv.at[n, o], term_peer(dyl, dz))

    def second_hop(buf, n, dx, dyh, dc, arrival):
        o = dx * 4 + dyh * 2 + dc
        slot = (((x - dx + 4) % 4) * 2 + (yh + dyh) % 2) * 2 + (c + dc) % 2 if arrival else sector
        ref = buf.at[slot]
        return remote(ref, ref, s_send.at[n, o], s_recv.at[n, o], sector_peer(dx, dyh, dc))

    def sum_start(bufs, n, value):
        bufs[0][term] = value
        for o in term_offsets:
            first_hop(bufs[0], n, *o, False).start()

    def sum_forward(bufs, n):
        for o in term_offsets:
            first_hop(bufs[0], n, *o, True).wait_recv()
        bufs[1][sector] = jnp.sum(bufs[0][...], axis=0)
        for o in sector_offsets:
            second_hop(bufs[1], n + 1, *o, False).start()

    def sum_finish(bufs, n):
        for o in sector_offsets:
            second_hop(bufs[1], n + 1, *o, True).wait_recv()
        for o in term_offsets:
            first_hop(bufs[0], n, *o, False).wait_send()
        for o in sector_offsets:
            second_hop(bufs[1], n + 1, *o, False).wait_send()
        total = jnp.sum(bufs[1][...], axis=0)
        return jnp.sum(jnp.sum(total, axis=0, keepdims=True), axis=1, keepdims=True)

    quotient_sum = (qabuf, qbbuf)
    norm_sum = (nabuf, nbbuf)

    def scale_of(total):
        return 1.0 / jnp.sqrt(total / (16 * B * B) + EPSILON)

    z_start()
    sum_start(norm_sum, 2, spread(cur[...] * cur[...]))
    for move in moves[1:]:
        move.wait()

    def application(i, carry):
        for dz in range(1, 8):
            z_arrival(dz).wait_recv()
            z_copy(dz).wait_send()
        set_wave(zimg[...].astype(jnp.float32))
        gather(functools.partial(sum_forward, norm_sum, 2))
        total = sum_finish(norm_sum, 2)
        scale = jnp.where(i == 0, 1.0, scale_of(total))
        compute()
        applied = img[...] * scale
        overlap = spread(wave[sector].astype(jnp.float32) * applied)
        sum_start(quotient_sum, 0, overlap)
        pimg[...] = applied.reshape(16, SHARE, B).astype(jnp.bfloat16)
        for o in term_offsets:
            rs_copy(*o).start()
        rsbuf[term] = jnp.zeros((SHARE, B), jnp.bfloat16)
        now = cur[...] * scale
        partial = img[my_rows, :] * scale - beta[i] * prev[...]
        prev[...] = now
        sum_forward(quotient_sum, 0)
        for o in term_offsets:
            rs_arrival(*o).wait_recv()
        for t in range(16):
            partial = partial + rsbuf[t].astype(jnp.float32)
        quotient = sum_finish(quotient_sum, 0) / (total * scale)
        residual = diag[...] * (partial - quotient * now)
        cur[...] = residual

        @pl.when(i < APPS - 1)
        def _():
            zimg[z] = residual.astype(jnp.bfloat16)
            z_start()

        sum_start(norm_sum, 2, spread(residual * residual))
        ray_ref[i] = jnp.sum(quotient)
        for o in term_offsets:
            rs_copy(*o).wait_send()
        return carry

    lax.fori_loop(0, APPS, application, 0)
    sum_forward(norm_sum, 2)
    out_ref[0] = cur[...] * scale_of(sum_finish(norm_sum, 2))


def local(x_start, x_prev, precond, left_env, right_env, triples, trip_count, term_coef, lanczos_beta, block_owner):
    vmem = pl.BlockSpec(memory_space=pltpu.VMEM)
    smem = pl.BlockSpec(memory_space=pltpu.SMEM)
    hbm = pl.BlockSpec(memory_space=pltpu.HBM)
    dma = pltpu.SemaphoreType.DMA
    f32, bf16 = jnp.float32, jnp.bfloat16
    return pl.pallas_call(
        kernel,
        out_shape=(jax.ShapeDtypeStruct((1, SHARE, B), f32), jax.ShapeDtypeStruct((APPS,), f32)),
        in_specs=[hbm] * 10,
        out_specs=(vmem, smem),
        scratch_shapes=[
            pltpu.VMEM((8, B, B), bf16),
            pltpu.VMEM((8, B, B), bf16),
            pltpu.VMEM((16, B, B), bf16),
            pltpu.VMEM((B, GROUP * B), bf16),
            pltpu.VMEM((B, B), f32),
            pltpu.VMEM((16, SHARE, B), bf16),
            pltpu.VMEM((16, SHARE, B), bf16),
            pltpu.VMEM((8, SHARE, B), bf16),
            pltpu.VMEM((SHARE, B), f32),
            pltpu.VMEM((SHARE, B), f32),
            pltpu.VMEM((SHARE, B), f32),
            pltpu.VMEM((16, 8, 128), f32),
            pltpu.VMEM((16, 8, 128), f32),
            pltpu.VMEM((16, 8, 128), f32),
            pltpu.VMEM((16, 8, 128), f32),
            pltpu.SMEM((4, TRIP), jnp.int32),
            pltpu.SMEM((1,), jnp.int32),
            pltpu.SMEM((64,), f32),
            pltpu.SMEM((APPS,), f32),
            pltpu.SMEM((16,), jnp.int32),
            dma((10,)),
            dma((20,)),
            dma((20,)),
            dma((16,)),
            dma((16,)),
            dma((16,)),
            dma((16,)),
            dma((8,)),
            dma((8,)),
            dma((4, 16)),
            dma((4, 16)),
        ],
        compiler_params=pltpu.CompilerParams(
            collective_id=0, has_side_effects=True, vmem_limit_bytes=64 * 2**20
        ),
        name="window",
    )(x_start, x_prev, precond, left_env, right_env, triples.T, trip_count.reshape(1), term_coef, lanczos_beta, block_owner)


def solution(mesh):
    torus = Mesh(mesh.devices.reshape(4, 2, 2, 2, 8), ALL)
    return jax.shard_map(
        local,
        mesh=torus,
        in_specs=(
            P(SECTOR, TERM, None),
            P(SECTOR, TERM, None),
            P(SECTOR, TERM, None),
            P(ALL, None, None),
            P(ALL, None, None),
            P(ALL, None),
            P(SECTOR, TERM),
            P(),
            P(),
            P(),
        ),
        out_specs=(P(SECTOR, TERM, None), P()),
        check_vma=False,
    )
```

time: 181 us -> 169 us (0.934)
  local copies, waits for them, and re-layouts: 9.5 us -> 2.53 us
  Pallas kernels: 170 us -> 165 us
    unnamed x19 -> x2, local copies, waits for them, and re-layouts: 9.5 us -> 2.53 us
    pallas_call x1, Pallas kernels: 170 us -> 165 us  [local(): pl.pallas_call(kernel, out_shape=(jax.ShapeDtypeStruct((1, SHARE, B), f32...]
where the time goes in v2:
time: 169 us
  Pallas kernels  165 us (98%)
  local copies, waits for them, and re-layouts  2.53 us (1%)
    pallas_call x1, Pallas kernels, local(): pl.pallas_call(kernel, out_shape=(jax.ShapeDtypeStruct((1, SHARE, B), f32...  165 us

profile of v2, /device:TPU:1, one launch (start us, length us, event | category | flops | bytes accessed | tf_op | source)
XLA Modules:
  0.0 169.2 jit_solution(11318477260614818691)
XLA Ops:
  1.3 165.4 %window.1 = (f32[1,24,384]{2,1,0:T(8,128)}, f32[3]{0:T(128)}) custom-call(f32[1,24,384]{2,1,0:T(8,128)} %x_hbm.1, f32[1,24,384]{2,1,0:T(8,128)} %xp_hbm.1, f32[1,24,384]{2,1,0:T(8,128)} %d_hbm.1, bf16[8,384,384]{2,1,0:T(8,128)(2,1)} %left_hbm.1, bf16[8,384,384]{2,1,0:T(8,128)(2,1)} %right_hbm.1, s32[4,20]{1,0:T(4,128)} %bitcast.3, s32[1]{0:T(128)} %bitcast.2.count_hbm, ...), custom_call_target="tpu_custom_call" | custom-call | tf_op jit(solution)/shard_map/window/pallas_call | solution.py:381
  166.7 1.4 copy.15
  168.1 1.1 copy.16

commit v3 on v2

--- a/solution.py
+++ b/solution.py
@@ -1,4 +1,3 @@
-import functools
 import math
 
 import jax
@@ -15,7 +14,7 @@
 SHARE = 24
 PIECE = 192
 HALF = 96
-GROUP = 4
+GROUP = 10
 SECTOR = ("x", "yh", "c")
 TERM = ("yl", "z")
 ALL = ("x", "yh", "c", "yl", "z")
@@ -45,6 +44,11 @@
     pimg,
     rsbuf,
     zimg,
+    zcur,
+    zprev,
+    zdiag,
+    scale,
+    ray_now,
     cur,
     prev,
     diag,
@@ -68,6 +72,8 @@
     z_recv,
     s_send,
     s_recv,
+    i_send,
+    i_recv,
 ):
     x = lax.axis_index("x")
     yh = lax.axis_index("yh")
@@ -125,13 +131,13 @@
         move.start()
 
     barrier = pltpu.get_barrier_semaphore()
-    peers = [term_peer(*o) for o in term_offsets] + [sector_peer(*o) for o in sector_offsets]
-    peers.append({"x": x, "yh": 1 - yh, "c": c, "yl": 1 - yl, "z": z})
+    peers = [term_peer(0, dz) for dz in range(1, 8)] + [along_p(1), along_p(-1), along_p(2)]
+    peers += [along_q(1), along_q(-1), sibling]
     for dev in peers:
         pl.semaphore_signal(barrier, inc=1, device_id=dev, device_id_type=MESH)
-    my_rows = pl.ds(pl.multiple_of(SHARE * term, 8), SHARE)
     moves[0].wait()
     zimg[z] = cur[...].astype(jnp.bfloat16)
+    scale[...] = jnp.ones_like(scale)
     pl.semaphore_wait(barrier, len(peers))
 
     def z_copy(dz):
@@ -149,6 +155,28 @@
     def set_wave(value):
         rows = pl.ds(pl.multiple_of(PIECE * yl, 64), PIECE)
         wave[sector, rows, :] = value.reshape(PIECE, B).astype(jnp.bfloat16)
+
+    states = ((0, zcur), (1, zprev), (2, zdiag))
+
+    def state_copy(n, dz):
+        mine = states[n][1].at[z]
+        return remote(mine, mine, i_send.at[n, dz], i_recv.at[n, dz], term_peer(0, dz))
+
+    def state_arrival(n, dz):
+        theirs = states[n][1].at[(z - dz + 8) % 8]
+        return remote(theirs, theirs, i_send.at[n, dz], i_recv.at[n, dz], term_peer(0, dz))
+
+    def state_start():
+        for n, own in enumerate((cur, prev, diag)):
+            states[n][1][z] = own[...]
+            for dz in range(1, 8):
+                state_copy(n, dz).start()
+
+    def state_finish():
+        for n in range(3):
+            for dz in range(1, 8):
+                state_arrival(n, dz).wait_recv()
+                state_copy(n, dz).wait_send()
 
     def piece_at(px, py, core, start, length):
         block = (px * 2 + py // 2) * 2 + core
@@ -160,14 +188,12 @@
         return piece_at((1 - c) * b + c * a, (1 - c) * a + c * b, c, start, length)
 
     def p_copy(k):
-        where = (piece(p, q), piece(p, q), piece(p - 1, q, 0, HALF), piece(p + 1, q, HALF, HALF))[k]
-        dev = along_p(1 if k % 2 == 0 else -1)
-        return remote(where, where, g_send.at[k], g_recv.at[k], dev)
+        where = piece(p, q)
+        return remote(where, where, g_send.at[k], g_recv.at[k], along_p((1, -1, 2)[k]))
 
     def p_arrival(k):
-        where = (piece(p - 1, q), piece(p + 1, q), piece(p - 2, q, 0, HALF), piece(p + 2, q, HALF, HALF))[k]
-        dev = along_p(1 if k % 2 == 0 else -1)
-        return remote(where, where, g_send.at[k], g_recv.at[k], dev)
+        where = piece(p - (1, -1, 2)[k], q)
+        return remote(where, where, g_send.at[k], g_recv.at[k], along_p((1, -1, 2)[k]))
 
     def q_copy(j, k):
         a = p + OFFSETS[j]
@@ -199,15 +225,15 @@
         return remote(where, where, b_send.at[n], b_recv.at[n], sibling)
 
     def gather(beside):
-        p_copy(0).start()
-        p_copy(1).start()
+        for k in range(3):
+            p_copy(k).start()
         q_copy(0, 0).start()
         q_copy(0, 1).start()
         to_sibling(p, q).start()
-        for k in (0, 1):
-            p_arrival(k).wait_recv()
-            p_copy(2 + k).start()
-        for j in (1, 2):
+        beside()
+
+        def column(j):
+            p_arrival(j - 1).wait_recv()
             q_copy(j, 0).start()
             q_copy(j, 1).start()
             to_sibling(p + OFFSETS[j], q).start()
@@ -219,39 +245,37 @@
             to_sibling(p + OFFSETS[j], q - 1).start()
             to_sibling(p + OFFSETS[j], q + 1).start()
 
-        neighbours(0)
-        p_arrival(2).wait_recv()
-        p_arrival(3).wait_recv()
-        q_copy(3, 0).start()
-        q_copy(3, 1).start()
-        to_sibling(p + 2, q).start()
-
         def opposite(j):
             q_arrival(j, 2).wait_recv()
             q_arrival(j, 3).wait_recv()
             to_sibling(p + OFFSETS[j], q + 2).start()
 
+        column(1)
+        column(2)
+        neighbours(0)
+        column(3)
         neighbours(1)
         neighbours(2)
-        beside()
         opposite(0)
         neighbours(3)
         opposite(1)
         opposite(2)
         opposite(3)
-        for k in range(4):
+        for n in range(16):
+            from_sibling(n).wait_recv()
+
+    def gather_sent():
+        for k in range(3):
             p_copy(k).wait_send()
         for j in range(4):
             for k in range(4):
                 q_copy(j, k).wait_send()
         for n in range(16):
-            from_sibling(n).wait_recv()
-        for n in range(16):
             sent_to_sibling(n).wait_send()
 
     normaliser = 1.0 / math.sqrt(16 * TRIP)
 
-    def compute():
+    def compute(rows):
         live = count[0]
         img[...] = jnp.zeros_like(img)
 
@@ -260,7 +284,9 @@
                 k = g * GROUP + j
                 weight = jnp.where(k < live, coef[triples[3, k]] * normaliser, 0.0)
                 m = jnp.dot(
-                    left[triples[0, k]], wave[owner[triples[1, k]]], preferred_element_type=jnp.float32
+                    left[triples[0, k], rows, :],
+                    wave[owner[triples[1, k]]],
+                    preferred_element_type=jnp.float32,
                 )
                 mid[:, j * B : (j + 1) * B] = (m * weight).astype(jnp.bfloat16)
             rights = jnp.concatenate([right[triples[2, g * GROUP + j]] for j in range(GROUP)], axis=0)
@@ -280,7 +306,7 @@
         return remote(rsbuf.at[sender], rsbuf.at[sender], r_send.at[o], r_recv.at[o], term_peer(dyl, dz))
 
     def spread(value):
-        rows = jnp.sum(value.reshape(-1, 8, B), axis=0)
+        rows = jnp.sum(jnp.sum(value.reshape(-1, 8, B), axis=0), axis=0, keepdims=True)
         return rows[:, :128] + rows[:, 128:256] + rows[:, 256:]
 
     def first_hop(buf, n, dyl, dz, arrival):
@@ -296,7 +322,7 @@
         return remote(ref, ref, s_send.at[n, o], s_recv.at[n, o], sector_peer(dx, dyh, dc))
 
     def sum_start(bufs, n, value):
-        bufs[0][term] = value
+        bufs[0][term] = jnp.concatenate(value + [jnp.zeros((8 - len(value), 128), jnp.float32)], axis=0)
         for o in term_offsets:
             first_hop(bufs[0], n, *o, False).start()
 
@@ -310,66 +336,139 @@
     def sum_finish(bufs, n):
         for o in sector_offsets:
             second_hop(bufs[1], n + 1, *o, True).wait_recv()
+        return jnp.sum(jnp.sum(bufs[1][...], axis=0), axis=1, keepdims=True)
+
+    def sum_sent(bufs, n):
         for o in term_offsets:
             first_hop(bufs[0], n, *o, False).wait_send()
         for o in sector_offsets:
             second_hop(bufs[1], n + 1, *o, False).wait_send()
-        total = jnp.sum(bufs[1][...], axis=0)
-        return jnp.sum(jnp.sum(total, axis=0, keepdims=True), axis=1, keepdims=True)
 
     quotient_sum = (qabuf, qbbuf)
     norm_sum = (nabuf, nbbuf)
 
-    def scale_of(total):
-        return 1.0 / jnp.sqrt(total / (16 * B * B) + EPSILON)
+    def norm_scale(i):
+        totals = sum_finish(norm_sum, 2)
+        ii, ic, ip, cc, cp, pp = [totals[j : j + 1] for j in range(6)]
+        quotient = ray_now[...]
+        beta_now = beta[i]
+        squares = (
+            ii
+            - 2.0 * quotient * ic
+            - 2.0 * beta_now * ip
+            + quotient * quotient * cc
+            + 2.0 * quotient * beta_now * cp
+            + beta_now * beta_now * pp
+        )
+        return 1.0 / jnp.sqrt(squares / (16 * B * B) + EPSILON)
 
     z_start()
-    sum_start(norm_sum, 2, spread(cur[...] * cur[...]))
     for move in moves[1:]:
         move.wait()
+    for dz in range(1, 8):
+        z_arrival(dz).wait_recv()
+        z_copy(dz).wait_send()
+    set_wave(zimg[...].astype(jnp.float32))
+    own_rows = pl.ds(pl.multiple_of(PIECE * yl, 64), PIECE)
+    other_rows = pl.ds(pl.multiple_of(PIECE * (1 - yl), 64), PIECE)
+    share_rows = pl.ds(pl.multiple_of(SHARE * z, 8), SHARE)
 
     def application(i, carry):
+        def beside():
+            @pl.when(i == 0)
+            def _():
+                state_start()
+
+            @pl.when(i > 0)
+            def _():
+                sum_forward(norm_sum, 2)
+
+        gather(beside)
+
+        @pl.when(i > 0)
+        def _():
+            scale[...] = norm_scale(i - 1)
+
+        factor = scale[...]
+        compute(other_rows)
+        applied = img[...] * factor
+        overlap = spread(wave[sector, other_rows, :].astype(jnp.float32) * applied)
+        pimg[pl.ds((1 - yl) * 8, 8)] = applied.reshape(8, SHARE, B).astype(jnp.bfloat16)
+        for dz in range(8):
+            rs_copy(1, dz).start()
+        gather_sent()
+        compute(own_rows)
+        img[...] = img[...] * factor
+        applied = img[...]
+        overlap = overlap + spread(wave[sector, own_rows, :].astype(jnp.float32) * applied)
+        now = cur[...] * factor
+        sum_start(quotient_sum, 0, [overlap * factor, spread(now * now)])
+        pimg[pl.ds(yl * 8, 8)] = applied.reshape(8, SHARE, B).astype(jnp.bfloat16)
         for dz in range(1, 8):
-            z_arrival(dz).wait_recv()
-            z_copy(dz).wait_send()
-        set_wave(zimg[...].astype(jnp.float32))
-        gather(functools.partial(sum_forward, norm_sum, 2))
-        total = sum_finish(norm_sum, 2)
-        scale = jnp.where(i == 0, 1.0, scale_of(total))
-        compute()
-        applied = img[...] * scale
-        overlap = spread(wave[sector].astype(jnp.float32) * applied)
-        sum_start(quotient_sum, 0, overlap)
-        pimg[...] = applied.reshape(16, SHARE, B).astype(jnp.bfloat16)
-        for o in term_offsets:
-            rs_copy(*o).start()
+            rs_copy(0, dz).start()
         rsbuf[term] = jnp.zeros((SHARE, B), jnp.bfloat16)
-        now = cur[...] * scale
-        partial = img[my_rows, :] * scale - beta[i] * prev[...]
-        prev[...] = now
+
+        @pl.when(i == 0)
+        def _():
+            state_finish()
+
+        @pl.when(i > 0)
+        def _():
+            sum_sent(norm_sum, 2)
+            zcur[...] = zcur[...] * factor
+
+        before = prev[...]
+        square = diag[...] * diag[...]
+        squared_now = square * now
+        squared_before = square * before
+        fixed = [spread(squared_now * now), spread(squared_now * before), spread(squared_before * before)]
         sum_forward(quotient_sum, 0)
         for o in term_offsets:
             rs_arrival(*o).wait_recv()
+        image = img[share_rows, :]
         for t in range(16):
-            partial = partial + rsbuf[t].astype(jnp.float32)
-        quotient = sum_finish(quotient_sum, 0) / (total * scale)
-        residual = diag[...] * (partial - quotient * now)
-        cur[...] = residual
+            image = image + rsbuf[t].astype(jnp.float32)
 
         @pl.when(i < APPS - 1)
         def _():
-            zimg[z] = residual.astype(jnp.bfloat16)
+            zimg[z] = image.astype(jnp.bfloat16)
             z_start()
 
-        sum_start(norm_sum, 2, spread(residual * residual))
-        ray_ref[i] = jnp.sum(quotient)
+        squared_image = square * image
+        sum_start(
+            norm_sum,
+            2,
+            [spread(squared_image * image), spread(squared_now * image), spread(squared_before * image)] + fixed,
+        )
         for o in term_offsets:
             rs_copy(*o).wait_send()
+        totals = sum_finish(quotient_sum, 0)
+        quotient = totals[0:1] / totals[1:2]
+        ray_now[...] = quotient
+        beta_now = beta[i]
+
+        @pl.when(i < APPS - 1)
+        def _():
+            for dz in range(1, 8):
+                z_arrival(dz).wait_recv()
+            znow = zcur[...]
+            znext = zdiag[...] * (zimg[...].astype(jnp.float32) - quotient * znow - beta_now * zprev[...])
+            set_wave(znext)
+            zprev[...] = znow
+            zcur[...] = znext
+            for dz in range(1, 8):
+                z_copy(dz).wait_send()
+
+        cur[...] = diag[...] * (image - quotient * now - beta_now * before)
+        prev[...] = now
+        ray_ref[i] = jnp.sum(quotient)
+        sum_sent(quotient_sum, 0)
         return carry
 
     lax.fori_loop(0, APPS, application, 0)
     sum_forward(norm_sum, 2)
-    out_ref[0] = cur[...] * scale_of(sum_finish(norm_sum, 2))
+    out_ref[0] = cur[...] * norm_scale(APPS - 1)
+    sum_sent(norm_sum, 2)
 
 
 def local(x_start, x_prev, precond, left_env, right_env, triples, trip_count, term_coef, lanczos_beta, block_owner):
@@ -387,11 +486,16 @@
             pltpu.VMEM((8, B, B), bf16),
             pltpu.VMEM((8, B, B), bf16),
             pltpu.VMEM((16, B, B), bf16),
-            pltpu.VMEM((B, GROUP * B), bf16),
-            pltpu.VMEM((B, B), f32),
+            pltpu.VMEM((PIECE, GROUP * B), bf16),
+            pltpu.VMEM((PIECE, B), f32),
             pltpu.VMEM((16, SHARE, B), bf16),
             pltpu.VMEM((16, SHARE, B), bf16),
             pltpu.VMEM((8, SHARE, B), bf16),
+            pltpu.VMEM((8, SHARE, B), f32),
+            pltpu.VMEM((8, SHARE, B), f32),
+            pltpu.VMEM((8, SHARE, B), f32),
+            pltpu.VMEM((1, 1), f32),
+            pltpu.VMEM((1, 1), f32),
             pltpu.VMEM((SHARE, B), f32),
             pltpu.VMEM((SHARE, B), f32),
             pltpu.VMEM((SHARE, B), f32),
@@ -415,6 +519,8 @@
             dma((8,)),
             dma((4, 16)),
             dma((4, 16)),
+            dma((3, 8)),
+            dma((3, 8)),
         ],
         compiler_params=pltpu.CompilerParams(
             collective_id=0, has_side_effects=True, vmem_limit_bytes=64 * 2**20

time: 169 us -> 156 us (0.923)
  Pallas kernels: 165 us -> 152 us
    pallas_call x1, Pallas kernels: 165 us -> 152 us  [local(): pl.pallas_call(kernel, out_shape=(jax.ShapeDtypeStruct((1, SHARE, B), f32...]
where the time goes in v3:
time: 156 us
  Pallas kernels  152 us (97%)
  local copies, waits for them, and re-layouts  2.53 us (2%)
    pallas_call x1, Pallas kernels, local(): pl.pallas_call(kernel, out_shape=(jax.ShapeDtypeStruct((1, SHARE, B), f32...  152 us

profile of v3, /device:TPU:1, one launch (start us, length us, event | category | flops | bytes accessed | tf_op | source)
XLA Modules:
  0.0 155.6 jit_solution(9111661204850948356)
XLA Ops:
  1.3 151.7 %window.1 = (f32[1,24,384]{2,1,0:T(8,128)}, f32[3]{0:T(128)}) custom-call(f32[1,24,384]{2,1,0:T(8,128)} %x_hbm.1, f32[1,24,384]{2,1,0:T(8,128)} %xp_hbm.1, f32[1,24,384]{2,1,0:T(8,128)} %d_hbm.1, bf16[8,384,384]{2,1,0:T(8,128)(2,1)} %left_hbm.1, bf16[8,384,384]{2,1,0:T(8,128)(2,1)} %right_hbm.1, s32[4,20]{1,0:T(4,128)} %bitcast.3, s32[1]{0:T(128)} %bitcast.2.count_hbm, ...), custom_call_target="tpu_custom_call" | custom-call | tf_op jit(solution)/shard_map/window/pallas_call | solution.py:480
  153.0 1.4 copy.15
  154.4 1.1 copy.16

commit v4 on v3

--- a/solution.py
+++ b/solution.py
@@ -64,6 +64,7 @@
     in_sem,
     g_send,
     g_recv,
+    q_send,
     b_send,
     b_recv,
     r_send,
@@ -142,11 +143,12 @@
 
     def z_copy(dz):
         mine = zimg.at[z]
-        return remote(mine, mine, z_send.at[dz], z_recv.at[dz], term_peer(0, dz))
-
-    def z_arrival(dz):
-        theirs = zimg.at[(z - dz + 8) % 8]
-        return remote(theirs, theirs, z_send.at[dz], z_recv.at[dz], term_peer(0, dz))
+        return remote(mine, mine, z_send, z_recv, term_peer(0, dz))
+
+    def all_of(ref, length, send, recv):
+        return remote(ref.at[pl.ds(0, length)], ref.at[pl.ds(0, length)], send, recv, sibling)
+
+    z_all = all_of(zimg, 7, z_send, z_recv)
 
     def z_start():
         for dz in range(1, 8):
@@ -160,11 +162,7 @@
 
     def state_copy(n, dz):
         mine = states[n][1].at[z]
-        return remote(mine, mine, i_send.at[n, dz], i_recv.at[n, dz], term_peer(0, dz))
-
-    def state_arrival(n, dz):
-        theirs = states[n][1].at[(z - dz + 8) % 8]
-        return remote(theirs, theirs, i_send.at[n, dz], i_recv.at[n, dz], term_peer(0, dz))
+        return remote(mine, mine, i_send.at[n], i_recv.at[n], term_peer(0, dz))
 
     def state_start():
         for n, own in enumerate((cur, prev, diag)):
@@ -174,9 +172,9 @@
 
     def state_finish():
         for n in range(3):
-            for dz in range(1, 8):
-                state_arrival(n, dz).wait_recv()
-                state_copy(n, dz).wait_send()
+            everything = all_of(states[n][1], 7, i_send.at[n], i_recv.at[n])
+            everything.wait_recv()
+            everything.wait_send()
 
     def piece_at(px, py, core, start, length):
         block = (px * 2 + py // 2) * 2 + core
@@ -199,30 +197,25 @@
         a = p + OFFSETS[j]
         where = (piece(a, q), piece(a, q), piece(a, q - 1, 0, HALF), piece(a, q + 1, HALF, HALF))[k]
         dev = along_q(1 if k % 2 == 0 else -1)
-        n = 4 + 4 * j + k
-        return remote(where, where, g_send.at[n], g_recv.at[n], dev)
+        n = 3 + 4 * j + k
+        if j == 3 and k == 2:
+            where, dev = piece(a, q), along_q(2)
+        return remote(where, where, q_send, g_recv.at[n], dev)
 
     def q_arrival(j, k):
         a = p + OFFSETS[j]
         where = (piece(a, q - 1), piece(a, q + 1), piece(a, q - 2, 0, HALF), piece(a, q + 2, HALF, HALF))[k]
         dev = along_q(1 if k % 2 == 0 else -1)
-        n = 4 + 4 * j + k
-        return remote(where, where, g_send.at[n], g_recv.at[n], dev)
+        n = 3 + 4 * j + k
+        if j == 3 and k == 2:
+            where, dev = piece(a, q - 2), along_q(2)
+        return remote(where, where, q_send, g_recv.at[n], dev)
 
     def to_sibling(a, b):
-        a, b = (a + 4) % 4, (b + 4) % 4
-        px, py = (1 - c) * b + c * a, (1 - c) * a + c * b
-        where = piece_at(px, py, c, 0, PIECE)
-        n = px * 4 + py
-        return remote(where, where, b_send.at[n], b_recv.at[n], sibling)
-
-    def from_sibling(n):
-        where = piece_at(n // 4, n % 4, 1 - c, 0, PIECE)
-        return remote(where, where, b_send.at[n], b_recv.at[n], sibling)
-
-    def sent_to_sibling(n):
-        where = piece_at(n // 4, n % 4, c, 0, PIECE)
-        return remote(where, where, b_send.at[n], b_recv.at[n], sibling)
+        where = piece(a, b)
+        return remote(where, where, b_send, b_recv, sibling)
+
+    half_of_all = all_of(wave, 8, b_send, b_recv)
 
     def gather(beside):
         for k in range(3):
@@ -236,18 +229,22 @@
             p_arrival(j - 1).wait_recv()
             q_copy(j, 0).start()
             q_copy(j, 1).start()
+            if j == 3:
+                q_copy(j, 2).start()
             to_sibling(p + OFFSETS[j], q).start()
 
         def neighbours(j):
             for k in (0, 1):
                 q_arrival(j, k).wait_recv()
-                q_copy(j, 2 + k).start()
+                if j < 3:
+                    q_copy(j, 2 + k).start()
             to_sibling(p + OFFSETS[j], q - 1).start()
             to_sibling(p + OFFSETS[j], q + 1).start()
 
         def opposite(j):
             q_arrival(j, 2).wait_recv()
-            q_arrival(j, 3).wait_recv()
+            if j < 3:
+                q_arrival(j, 3).wait_recv()
             to_sibling(p + OFFSETS[j], q + 2).start()
 
         column(1)
@@ -261,17 +258,13 @@
         opposite(1)
         opposite(2)
         opposite(3)
-        for n in range(16):
-            from_sibling(n).wait_recv()
+        half_of_all.wait_recv()
 
     def gather_sent():
         for k in range(3):
             p_copy(k).wait_send()
-        for j in range(4):
-            for k in range(4):
-                q_copy(j, k).wait_send()
-        for n in range(16):
-            sent_to_sibling(n).wait_send()
+        all_of(wave, 6, q_send, b_recv).wait_send()
+        half_of_all.wait_send()
 
     normaliser = 1.0 / math.sqrt(16 * TRIP)
 
@@ -297,52 +290,32 @@
 
     def rs_copy(dyl, dz):
         to = ((yl + dyl) % 2) * 8 + (z + dz) % 8
-        o = dyl * 8 + dz
-        return remote(pimg.at[to], rsbuf.at[term], r_send.at[o], r_recv.at[o], term_peer(dyl, dz))
-
-    def rs_arrival(dyl, dz):
-        sender = ((yl + dyl) % 2) * 8 + (z - dz + 8) % 8
-        o = dyl * 8 + dz
-        return remote(rsbuf.at[sender], rsbuf.at[sender], r_send.at[o], r_recv.at[o], term_peer(dyl, dz))
+        return remote(pimg.at[to], rsbuf.at[term], r_send, r_recv, term_peer(dyl, dz))
 
     def spread(value):
         rows = jnp.sum(jnp.sum(value.reshape(-1, 8, B), axis=0), axis=0, keepdims=True)
         return rows[:, :128] + rows[:, 128:256] + rows[:, 256:]
 
-    def first_hop(buf, n, dyl, dz, arrival):
-        o = dyl * 8 + dz
-        slot = ((yl + dyl) % 2) * 8 + (z - dz + 8) % 8 if arrival else term
-        ref = buf.at[slot]
-        return remote(ref, ref, s_send.at[n, o], s_recv.at[n, o], term_peer(dyl, dz))
-
-    def second_hop(buf, n, dx, dyh, dc, arrival):
-        o = dx * 4 + dyh * 2 + dc
-        slot = (((x - dx + 4) % 4) * 2 + (yh + dyh) % 2) * 2 + (c + dc) % 2 if arrival else sector
-        ref = buf.at[slot]
-        return remote(ref, ref, s_send.at[n, o], s_recv.at[n, o], sector_peer(dx, dyh, dc))
-
     def sum_start(bufs, n, value):
-        bufs[0][term] = jnp.concatenate(value + [jnp.zeros((8 - len(value), 128), jnp.float32)], axis=0)
+        mine = bufs[0].at[term]
+        mine[...] = jnp.concatenate(value + [jnp.zeros((8 - len(value), 128), jnp.float32)], axis=0)
         for o in term_offsets:
-            first_hop(bufs[0], n, *o, False).start()
+            remote(mine, mine, s_send.at[n], s_recv.at[n], term_peer(*o)).start()
 
     def sum_forward(bufs, n):
-        for o in term_offsets:
-            first_hop(bufs[0], n, *o, True).wait_recv()
-        bufs[1][sector] = jnp.sum(bufs[0][...], axis=0)
+        all_of(bufs[0], 15, s_send.at[n], s_recv.at[n]).wait_recv()
+        mine = bufs[1].at[sector]
+        mine[...] = jnp.sum(bufs[0][...], axis=0)
         for o in sector_offsets:
-            second_hop(bufs[1], n + 1, *o, False).start()
+            remote(mine, mine, s_send.at[n + 1], s_recv.at[n + 1], sector_peer(*o)).start()
 
     def sum_finish(bufs, n):
-        for o in sector_offsets:
-            second_hop(bufs[1], n + 1, *o, True).wait_recv()
+        all_of(bufs[1], 15, s_send.at[n + 1], s_recv.at[n + 1]).wait_recv()
         return jnp.sum(jnp.sum(bufs[1][...], axis=0), axis=1, keepdims=True)
 
     def sum_sent(bufs, n):
-        for o in term_offsets:
-            first_hop(bufs[0], n, *o, False).wait_send()
-        for o in sector_offsets:
-            second_hop(bufs[1], n + 1, *o, False).wait_send()
+        all_of(bufs[0], 15, s_send.at[n], s_recv.at[n]).wait_send()
+        all_of(bufs[1], 15, s_send.at[n + 1], s_recv.at[n + 1]).wait_send()
 
     quotient_sum = (qabuf, qbbuf)
     norm_sum = (nabuf, nbbuf)
@@ -365,9 +338,8 @@
     z_start()
     for move in moves[1:]:
         move.wait()
-    for dz in range(1, 8):
-        z_arrival(dz).wait_recv()
-        z_copy(dz).wait_send()
+    z_all.wait_recv()
+    z_all.wait_send()
     set_wave(zimg[...].astype(jnp.float32))
     own_rows = pl.ds(pl.multiple_of(PIECE * yl, 64), PIECE)
     other_rows = pl.ds(pl.multiple_of(PIECE * (1 - yl), 64), PIECE)
@@ -423,8 +395,7 @@
         squared_before = square * before
         fixed = [spread(squared_now * now), spread(squared_now * before), spread(squared_before * before)]
         sum_forward(quotient_sum, 0)
-        for o in term_offsets:
-            rs_arrival(*o).wait_recv()
+        all_of(rsbuf, 15, r_send, r_recv).wait_recv()
         image = img[share_rows, :]
         for t in range(16):
             image = image + rsbuf[t].astype(jnp.float32)
@@ -440,8 +411,7 @@
             2,
             [spread(squared_image * image), spread(squared_now * image), spread(squared_before * image)] + fixed,
         )
-        for o in term_offsets:
-            rs_copy(*o).wait_send()
+        all_of(pimg, 15, r_send, r_recv).wait_send()
         totals = sum_finish(quotient_sum, 0)
         quotient = totals[0:1] / totals[1:2]
         ray_now[...] = quotient
@@ -449,15 +419,13 @@
 
         @pl.when(i < APPS - 1)
         def _():
-            for dz in range(1, 8):
-                z_arrival(dz).wait_recv()
+            z_all.wait_recv()
             znow = zcur[...]
             znext = zdiag[...] * (zimg[...].astype(jnp.float32) - quotient * znow - beta_now * zprev[...])
             set_wave(znext)
             zprev[...] = znow
             zcur[...] = znext
-            for dz in range(1, 8):
-                z_copy(dz).wait_send()
+            z_all.wait_send()
 
         cur[...] = diag[...] * (image - quotient * now - beta_now * before)
         prev[...] = now
@@ -509,18 +477,19 @@
             pltpu.SMEM((APPS,), f32),
             pltpu.SMEM((16,), jnp.int32),
             dma((10,)),
-            dma((20,)),
-            dma((20,)),
-            dma((16,)),
-            dma((16,)),
-            dma((16,)),
-            dma((16,)),
-            dma((8,)),
-            dma((8,)),
-            dma((4, 16)),
-            dma((4, 16)),
-            dma((3, 8)),
-            dma((3, 8)),
+            dma((3,)),
+            dma((19,)),
+            dma,
+            dma,
+            dma,
+            dma,
+            dma,
+            dma,
+            dma,
+            dma((4,)),
+            dma((4,)),
+            dma((3,)),
+            dma((3,)),
         ],
         compiler_params=pltpu.CompilerParams(
             collective_id=0, has_side_effects=True, vmem_limit_bytes=64 * 2**20

time: 156 us -> 150 us (0.962)
  Pallas kernels: 152 us -> 146 us
    pallas_call x1, Pallas kernels: 152 us -> 146 us  [local(): pl.pallas_call(kernel, out_shape=(jax.ShapeDtypeStruct((1, SHARE, B), f32...]
where the time goes in v4:
time: 150 us
  Pallas kernels  146 us (97%)
  local copies, waits for them, and re-layouts  2.53 us (2%)
    pallas_call x1, Pallas kernels, local(): pl.pallas_call(kernel, out_shape=(jax.ShapeDtypeStruct((1, SHARE, B), f32...  146 us

profile of v4, /device:TPU:1, one launch (start us, length us, event | category | flops | bytes accessed | tf_op | source)
XLA Modules:
  0.0 149.6 jit_solution(12429724418573003051)
XLA Ops:
  1.3 145.8 %window.1 = (f32[1,24,384]{2,1,0:T(8,128)}, f32[3]{0:T(128)}) custom-call(f32[1,24,384]{2,1,0:T(8,128)} %x_hbm.1, f32[1,24,384]{2,1,0:T(8,128)} %xp_hbm.1, f32[1,24,384]{2,1,0:T(8,128)} %d_hbm.1, bf16[8,384,384]{2,1,0:T(8,128)(2,1)} %left_hbm.1, bf16[8,384,384]{2,1,0:T(8,128)(2,1)} %right_hbm.1, s32[4,20]{1,0:T(4,128)} %bitcast.3, s32[1]{0:T(128)} %bitcast.2.count_hbm, ...), custom_call_target="tpu_custom_call" | custom-call | tf_op jit(solution)/shard_map/window/pallas_call | solution.py:448
  147.1 1.4 copy.15
  148.5 1.1 copy.16

commit v5 on v4

--- a/solution.py
+++ b/solution.py
@@ -14,7 +14,6 @@
 SHARE = 24
 PIECE = 192
 HALF = 96
-GROUP = 10
 SECTOR = ("x", "yh", "c")
 TERM = ("yl", "z")
 ALL = ("x", "yh", "c", "yl", "z")
@@ -52,6 +51,7 @@
     cur,
     prev,
     diag,
+    last,
     qabuf,
     qbbuf,
     nabuf,
@@ -102,8 +102,11 @@
     def sector_peer(dx, dyh, dc):
         return {"x": (x + dx) % 4, "yh": (yh + dyh) % 2, "c": (c + dc) % 2, "yl": yl, "z": z}
 
-    term_offsets = [(o // 8, o % 8) for o in range(1, 16)]
-    sector_offsets = [(o // 4, (o // 2) % 2, o % 2) for o in range(1, 16)]
+    ring = (4, 3, 5, 2, 6, 1, 7)
+    term_offsets = [(1, 4), (1, 3), (1, 5), (0, 4)] + [(1, 2), (1, 6), (0, 3), (0, 5), (1, 1), (1, 7)]
+    term_offsets += [(0, 2), (0, 6), (1, 0), (0, 1), (0, 7)]
+    sector_offsets = [(2, 1, 0), (2, 1, 1), (1, 1, 0), (1, 1, 1), (3, 1, 0), (3, 1, 1), (2, 0, 0), (2, 0, 1)]
+    sector_offsets += [(0, 1, 0), (0, 1, 1), (1, 0, 0), (1, 0, 1), (3, 0, 0), (3, 0, 1), (0, 0, 1)]
     sibling = sector_peer(0, 0, 1)
 
     def remote(src, dst, send, recv, dev):
@@ -132,7 +135,7 @@
         move.start()
 
     barrier = pltpu.get_barrier_semaphore()
-    peers = [term_peer(0, dz) for dz in range(1, 8)] + [along_p(1), along_p(-1), along_p(2)]
+    peers = [term_peer(0, dz) for dz in ring] + [along_p(1), along_p(-1), along_p(2)]
     peers += [along_q(1), along_q(-1), sibling]
     for dev in peers:
         pl.semaphore_signal(barrier, inc=1, device_id=dev, device_id_type=MESH)
@@ -151,7 +154,7 @@
     z_all = all_of(zimg, 7, z_send, z_recv)
 
     def z_start():
-        for dz in range(1, 8):
+        for dz in ring:
             z_copy(dz).start()
 
     def set_wave(value):
@@ -167,7 +170,7 @@
     def state_start():
         for n, own in enumerate((cur, prev, diag)):
             states[n][1][z] = own[...]
-            for dz in range(1, 8):
+            for dz in ring:
                 state_copy(n, dz).start()
 
     def state_finish():
@@ -270,23 +273,14 @@
 
     def compute(rows):
         live = count[0]
-        img[...] = jnp.zeros_like(img)
-
-        def step(g, carry):
-            for j in range(GROUP):
-                k = g * GROUP + j
-                weight = jnp.where(k < live, coef[triples[3, k]] * normaliser, 0.0)
-                m = jnp.dot(
-                    left[triples[0, k], rows, :],
-                    wave[owner[triples[1, k]]],
-                    preferred_element_type=jnp.float32,
-                )
-                mid[:, j * B : (j + 1) * B] = (m * weight).astype(jnp.bfloat16)
-            rights = jnp.concatenate([right[triples[2, g * GROUP + j]] for j in range(GROUP)], axis=0)
-            img[...] += jnp.dot(mid[...], rights, preferred_element_type=jnp.float32)
-            return carry
-
-        lax.fori_loop(0, TRIP // GROUP, step, 0)
+        for k in range(TRIP):
+            weight = jnp.where(k < live, coef[triples[3, k]] * normaliser, 0.0)
+            m = jnp.dot(
+                left[triples[0, k], rows, :], wave[owner[triples[1, k]]], preferred_element_type=jnp.float32
+            )
+            mid[:, k * B : (k + 1) * B] = (m * weight).astype(jnp.bfloat16)
+        rights = jnp.concatenate([right[triples[2, k]] for k in range(TRIP)], axis=0)
+        return jnp.dot(mid[...], rights, preferred_element_type=jnp.float32)
 
     def rs_copy(dyl, dz):
         to = ((yl + dyl) % 2) * 8 + (z + dz) % 8
@@ -298,7 +292,7 @@
 
     def sum_start(bufs, n, value):
         mine = bufs[0].at[term]
-        mine[...] = jnp.concatenate(value + [jnp.zeros((8 - len(value), 128), jnp.float32)], axis=0)
+        mine[...] = jnp.concatenate(value + [jnp.zeros((1, 128), jnp.float32)] * (8 - len(value)), axis=0)
         for o in term_offsets:
             remote(mine, mine, s_send.at[n], s_recv.at[n], term_peer(*o)).start()
 
@@ -320,10 +314,8 @@
     quotient_sum = (qabuf, qbbuf)
     norm_sum = (nabuf, nbbuf)
 
-    def norm_scale(i):
-        totals = sum_finish(norm_sum, 2)
+    def norm_scale(totals, quotient, i):
         ii, ic, ip, cc, cp, pp = [totals[j : j + 1] for j in range(6)]
-        quotient = ray_now[...]
         beta_now = beta[i]
         squares = (
             ii
@@ -359,24 +351,26 @@
 
         @pl.when(i > 0)
         def _():
-            scale[...] = norm_scale(i - 1)
+            scale[...] = norm_scale(sum_finish(norm_sum, 2), ray_now[...], i - 1)
 
         factor = scale[...]
-        compute(other_rows)
-        applied = img[...] * factor
+        applied = compute(other_rows) * factor
         overlap = spread(wave[sector, other_rows, :].astype(jnp.float32) * applied)
         pimg[pl.ds((1 - yl) * 8, 8)] = applied.reshape(8, SHARE, B).astype(jnp.bfloat16)
-        for dz in range(8):
+        for dz in ring + (0,):
             rs_copy(1, dz).start()
         gather_sent()
-        compute(own_rows)
-        img[...] = img[...] * factor
-        applied = img[...]
+        applied = compute(own_rows) * factor
+        img[...] = applied
         overlap = overlap + spread(wave[sector, own_rows, :].astype(jnp.float32) * applied)
         now = cur[...] * factor
-        sum_start(quotient_sum, 0, [overlap * factor, spread(now * now)])
+
+        @pl.when(i < APPS - 1)
+        def _():
+            sum_start(quotient_sum, 0, [overlap * factor, spread(now * now)])
+
         pimg[pl.ds(yl * 8, 8)] = applied.reshape(8, SHARE, B).astype(jnp.bfloat16)
-        for dz in range(1, 8):
+        for dz in ring:
             rs_copy(0, dz).start()
         rsbuf[term] = jnp.zeros((SHARE, B), jnp.bfloat16)
 
@@ -394,7 +388,11 @@
         squared_now = square * now
         squared_before = square * before
         fixed = [spread(squared_now * now), spread(squared_now * before), spread(squared_before * before)]
-        sum_forward(quotient_sum, 0)
+
+        @pl.when(i < APPS - 1)
+        def _():
+            sum_forward(quotient_sum, 0)
+
         all_of(rsbuf, 15, r_send, r_recv).wait_recv()
         image = img[share_rows, :]
         for t in range(16):
@@ -406,19 +404,27 @@
             z_start()
 
         squared_image = square * image
-        sum_start(
-            norm_sum,
-            2,
-            [spread(squared_image * image), spread(squared_now * image), spread(squared_before * image)] + fixed,
-        )
+        values = [spread(squared_image * image), spread(squared_now * image), spread(squared_before * image)]
+        values += fixed + [spread(now * image), spread(now * now)]
+
+        @pl.when(i < APPS - 1)
+        def _():
+            sum_start(norm_sum, 2, values)
+
+        @pl.when(i == APPS - 1)
+        def _():
+            sum_start(quotient_sum, 0, values)
+
         all_of(pimg, 15, r_send, r_recv).wait_send()
-        totals = sum_finish(quotient_sum, 0)
-        quotient = totals[0:1] / totals[1:2]
-        ray_now[...] = quotient
-        beta_now = beta[i]
+        cur[...] = now
+        last[...] = image
 
         @pl.when(i < APPS - 1)
         def _():
+            totals = sum_finish(quotient_sum, 0)
+            quotient = totals[0:1] / totals[1:2]
+            ray_now[...] = quotient
+            beta_now = beta[i]
             z_all.wait_recv()
             znow = zcur[...]
             znext = zdiag[...] * (zimg[...].astype(jnp.float32) - quotient * znow - beta_now * zprev[...])
@@ -427,16 +433,21 @@
             zcur[...] = znext
             z_all.wait_send()
 
-        cur[...] = diag[...] * (image - quotient * now - beta_now * before)
-        prev[...] = now
-        ray_ref[i] = jnp.sum(quotient)
-        sum_sent(quotient_sum, 0)
+            cur[...] = diag[...] * (image - quotient * now - beta_now * before)
+            prev[...] = now
+            ray_ref[i] = jnp.sum(quotient)
+            sum_sent(quotient_sum, 0)
+
         return carry
 
     lax.fori_loop(0, APPS, application, 0)
-    sum_forward(norm_sum, 2)
-    out_ref[0] = cur[...] * norm_scale(APPS - 1)
-    sum_sent(norm_sum, 2)
+    sum_forward(quotient_sum, 0)
+    totals = sum_finish(quotient_sum, 0)
+    quotient = totals[6:7] / totals[7:8]
+    residual = diag[...] * (last[...] - quotient * cur[...] - beta[APPS - 1] * prev[...])
+    out_ref[0] = residual * norm_scale(totals, quotient, APPS - 1)
+    ray_ref[APPS - 1] = jnp.sum(quotient)
+    sum_sent(quotient_sum, 0)
 
 
 def local(x_start, x_prev, precond, left_env, right_env, triples, trip_count, term_coef, lanczos_beta, block_owner):
@@ -454,7 +465,7 @@
             pltpu.VMEM((8, B, B), bf16),
             pltpu.VMEM((8, B, B), bf16),
             pltpu.VMEM((16, B, B), bf16),
-            pltpu.VMEM((PIECE, GROUP * B), bf16),
+            pltpu.VMEM((PIECE, TRIP * B), bf16),
             pltpu.VMEM((PIECE, B), f32),
             pltpu.VMEM((16, SHARE, B), bf16),
             pltpu.VMEM((16, SHARE, B), bf16),
@@ -464,6 +475,7 @@
             pltpu.VMEM((8, SHARE, B), f32),
             pltpu.VMEM((1, 1), f32),
             pltpu.VMEM((1, 1), f32),
+            pltpu.VMEM((SHARE, B), f32),
             pltpu.VMEM((SHARE, B), f32),
             pltpu.VMEM((SHARE, B), f32),
             pltpu.VMEM((SHARE, B), f32),

time: 150 us -> 142 us (0.947)
  Pallas kernels: 146 us -> 138 us
    pallas_call x1, Pallas kernels: 146 us -> 138 us  [local(): pl.pallas_call(kernel, out_shape=(jax.ShapeDtypeStruct((1, SHARE, B), f32...]
where the time goes in v5:
time: 142 us
  Pallas kernels  138 us (97%)
  local copies, waits for them, and re-layouts  2.53 us (2%)
    pallas_call x1, Pallas kernels, local(): pl.pallas_call(kernel, out_shape=(jax.ShapeDtypeStruct((1, SHARE, B), f32...  138 us

profile of v5, /device:TPU:1, one launch (start us, length us, event | category | flops | bytes accessed | tf_op | source)
XLA Modules:
  0.0 142.3 jit_solution(18412436733589012702)
XLA Ops:
  1.3 138.5 %window.1 = (f32[1,24,384]{2,1,0:T(8,128)}, f32[3]{0:T(128)}) custom-call(f32[1,24,384]{2,1,0:T(8,128)} %x_hbm.1, f32[1,24,384]{2,1,0:T(8,128)} %xp_hbm.1, f32[1,24,384]{2,1,0:T(8,128)} %d_hbm.1, bf16[8,384,384]{2,1,0:T(8,128)(2,1)} %left_hbm.1, bf16[8,384,384]{2,1,0:T(8,128)(2,1)} %right_hbm.1, s32[4,20]{1,0:T(4,128)} %bitcast.3, s32[1]{0:T(128)} %bitcast.2.count_hbm, ...), custom_call_target="tpu_custom_call" | custom-call | tf_op jit(solution)/shard_map/window/pallas_call | solution.py:459
  139.8 1.4 copy.15
  141.1 1.1 copy.16

commit v6 on v5

--- a/solution.py
+++ b/solution.py
@@ -226,7 +226,6 @@
         q_copy(0, 0).start()
         q_copy(0, 1).start()
         to_sibling(p, q).start()
-        beside()
 
         def column(j):
             p_arrival(j - 1).wait_recv()
@@ -252,6 +251,7 @@
 
         column(1)
         column(2)
+        beside()
         neighbours(0)
         column(3)
         neighbours(1)

time: 142 us -> 142 us (level)
  no operation moved by 1% of the time
where the time goes in v6:
time: 142 us; the launch traced here: 141 us
  Pallas kernels  138 us (97%)
  local copies, waits for them, and re-layouts  2.53 us (2%)
    pallas_call x1, Pallas kernels, local(): pl.pallas_call(kernel, out_shape=(jax.ShapeDtypeStruct((1, SHARE, B), f32...  138 us

profile of v6, /device:TPU:1, one launch (start us, length us, event | category | flops | bytes accessed | tf_op | source)
XLA Modules:
  0.0 141.4 jit_solution(13094658072064052432)
XLA Ops:
  1.3 137.6 %window.1 = (f32[1,24,384]{2,1,0:T(8,128)}, f32[3]{0:T(128)}) custom-call(f32[1,24,384]{2,1,0:T(8,128)} %x_hbm.1, f32[1,24,384]{2,1,0:T(8,128)} %xp_hbm.1, f32[1,24,384]{2,1,0:T(8,128)} %d_hbm.1, bf16[8,384,384]{2,1,0:T(8,128)(2,1)} %left_hbm.1, bf16[8,384,384]{2,1,0:T(8,128)(2,1)} %right_hbm.1, s32[4,20]{1,0:T(4,128)} %bitcast.3, s32[1]{0:T(128)} %bitcast.2.count_hbm, ...), custom_call_target="tpu_custom_call" | custom-call | tf_op jit(solution)/shard_map/window/pallas_call | solution.py:459
  138.9 1.4 copy.15
  140.3 1.1 copy.16
